TPU v7x, 32 devices: a whole 2x2x4 slice. The times are simulated.
32 devices in a mesh: space: 2 (over x), vel: 16 (over z, y, core).
Axes of the slice: x: 2, y: 2, z: 4, core: 2. Of those that a mesh axis runs over, the one named last changes fastest.
Arguments:
- distribution: float32 [8192, 512], P('vel', 'space'), may hold values from 0.1 to 32, as said below
- normals: float32 [4, 3, 512], P(None, None, 'space'), may hold values from -0.3 to 0.3
- adjacency: int32 [4, 512], P(None, 'space'), may hold values from 0 to 511, as said below
- send_list: int32 [2, 2, 256], P('space'), may hold values from 0 to 255
- block_counts: int32 [2, 2], P(None, 'space'), may hold values from 0 to 2, as said below
Outputs:
- relaxed: float32 [8192, 512], P('vel', 'space')
- fields: float32 [13, 512], P(None, 'space')
Inputs may be any that keep to these rules, and one draw needn't show every extreme that they name: `adjacency`: every entry of 256 or more names a position below 128 times the sum of block_counts over the senders to its group. `block_counts`: no group sends to itself; every other pair has at least one block; one receiving group gets 2 blocks from every other group. `distribution`: Positive.
All inputs are finite; a program needn't handle non-finite values.
Results may differ from a plain program's by a relative error of at most 0.00011.
Values sent between devices are 32-bit elements; how exact they have to be, the bound alone decides.
A program may use at most 64 MiB of HBM per device.

v0:
```python
import functools

import jax
import jax.numpy as jnp
from jax import lax
from jax.experimental import pallas as pl
from jax.experimental.pallas import tpu as pltpu
from jax.sharding import PartitionSpec as P

VXY = 32
TILE = 128
ITERS = 2


spacing = 0.3
ellipsoid_mix = -0.25
prandtl = 0.8
visc_power = 0.26
time_step = 0.025


def velocity_nodes(vel_index, z_count):
    comp_x = (vel_index % VXY).astype(jnp.float32)
    comp_y = (vel_index // VXY % VXY).astype(jnp.float32)
    comp_z = (vel_index // (VXY * VXY)).astype(jnp.float32)
    centre = (VXY - 1) / 2.0
    return jnp.stack(
        [
            (comp_x - centre) * spacing,
            (comp_y - centre) * spacing,
            (comp_z - (z_count - 1) / 2.0) * spacing,
        ]
    )


def moment_rows(velocity):
    comp_x, comp_y, comp_z = (velocity[0], velocity[1], velocity[2])
    squared = comp_x * comp_x + comp_y * comp_y + comp_z * comp_z
    return jnp.stack(
        [
            jnp.ones_like(comp_x),
            comp_x,
            comp_y,
            comp_z,
            comp_x * comp_x,
            comp_y * comp_y,
            comp_z * comp_z,
            comp_x * comp_y,
            comp_x * comp_z,
            comp_y * comp_z,
            comp_x * squared,
            comp_y * squared,
            comp_z * squared,
        ]
    )


def quad_rows(velocity):
    comp_x, comp_y, comp_z = (velocity[0], velocity[1], velocity[2])
    return jnp.stack(
        [
            comp_x * comp_x,
            comp_y * comp_y,
            comp_z * comp_z,
            comp_x * comp_y,
            comp_x * comp_z,
            comp_y * comp_z,
            comp_x,
            comp_y,
            comp_z,
            jnp.ones_like(comp_x),
        ]
    )


def macroscopic(moments):
    density = moments[0]
    mean_x = moments[1] / density
    mean_y = moments[2] / density
    mean_z = moments[3] / density
    second = moments[4:10] / density[None, :]
    third = moments[10:13] / density[None, :]
    theta_xx = second[0] - mean_x * mean_x
    theta_yy = second[1] - mean_y * mean_y
    theta_zz = second[2] - mean_z * mean_z
    theta_xy = second[3] - mean_x * mean_y
    theta_xz = second[4] - mean_x * mean_z
    theta_yz = second[5] - mean_y * mean_z
    temper = (theta_xx + theta_yy + theta_zz) / 3.0
    trace_b = second[0] + second[1] + second[2]
    bu_x = second[0] * mean_x + second[3] * mean_y + second[4] * mean_z
    bu_y = second[3] * mean_x + second[1] * mean_y + second[5] * mean_z
    bu_z = second[4] * mean_x + second[5] * mean_y + second[2] * mean_z
    mean_sq = mean_x * mean_x + mean_y * mean_y + mean_z * mean_z
    flux_x = 0.5 * (third[0] - 2.0 * bu_x - mean_x * trace_b + 2.0 * mean_x * mean_sq)
    flux_y = 0.5 * (third[1] - 2.0 * bu_y - mean_y * trace_b + 2.0 * mean_y * mean_sq)
    flux_z = 0.5 * (third[2] - 2.0 * bu_z - mean_z * trace_b + 2.0 * mean_z * mean_sq)
    iso_part = (1.0 - ellipsoid_mix) * temper
    lam_xx = iso_part + ellipsoid_mix * theta_xx
    lam_yy = iso_part + ellipsoid_mix * theta_yy
    lam_zz = iso_part + ellipsoid_mix * theta_zz
    lam_xy = ellipsoid_mix * theta_xy
    lam_xz = ellipsoid_mix * theta_xz
    lam_yz = ellipsoid_mix * theta_yz
    cof_xx = lam_yy * lam_zz - lam_yz * lam_yz
    cof_xy = lam_yz * lam_xz - lam_xy * lam_zz
    cof_xz = lam_xy * lam_yz - lam_yy * lam_xz
    cof_yy = lam_xx * lam_zz - lam_xz * lam_xz
    cof_yz = lam_xy * lam_xz - lam_xx * lam_yz
    cof_zz = lam_xx * lam_yy - lam_xy * lam_xy
    determinant = lam_xx * cof_xx + lam_xy * cof_xy + lam_xz * cof_xz
    inv_xx = cof_xx / determinant
    inv_yy = cof_yy / determinant
    inv_zz = cof_zz / determinant
    inv_xy = cof_xy / determinant
    inv_xz = cof_xz / determinant
    inv_yz = cof_yz / determinant
    lin_x = inv_xx * mean_x + inv_xy * mean_y + inv_xz * mean_z
    lin_y = inv_xy * mean_x + inv_yy * mean_y + inv_yz * mean_z
    lin_z = inv_xz * mean_x + inv_yz * mean_y + inv_zz * mean_z
    offset = mean_x * lin_x + mean_y * lin_y + mean_z * lin_z
    collide = prandtl * density * jnp.exp(visc_power * jnp.log(temper))
    return jnp.stack(
        [
            density,
            mean_x,
            mean_y,
            mean_z,
            theta_xx,
            theta_yy,
            theta_zz,
            theta_xy,
            theta_xz,
            theta_yz,
            flux_x,
            flux_y,
            flux_z,
            inv_xx,
            inv_yy,
            inv_zz,
            2.0 * inv_xy,
            2.0 * inv_xz,
            2.0 * inv_yz,
            -2.0 * lin_x,
            -2.0 * lin_y,
            -2.0 * lin_z,
            offset,
            collide,
        ]
    )


def ghost_slots(adjacency, counts, cells, groups, slot_count):
    ends = jnp.cumsum(counts) * TILE
    starts = ends - counts * TILE
    is_local = adjacency < cells
    position = jnp.maximum(adjacency - cells, 0)
    source = jnp.sum((ends[:, None, None] <= position[None]).astype(jnp.int32), axis=0)
    source = jnp.minimum(source, groups - 1)
    group_ids = jnp.arange(groups, dtype=jnp.int32)[:, None, None]
    chosen = jnp.sum(jnp.where(group_ids == source[None], starts[:, None, None], 0), axis=0)
    slot_pos = jnp.clip(position - chosen, 0, slot_count - 1)
    return (is_local, source, slot_pos)


def relax(current, neighbours, velocity, normals, params, norm_z, equilibrium):
    gauss = params[0][None, :] * equilibrium / norm_z[None, :]
    outflow = jnp.zeros(current.shape, jnp.float32)
    inflow = jnp.zeros(current.shape, jnp.float32)
    for side in range(normals.shape[0]):
        normal_speed = (
            velocity[0][:, None] * normals[side, 0][None, :]
            + velocity[1][:, None] * normals[side, 1][None, :]
            + velocity[2][:, None] * normals[side, 2][None, :]
        )
        outflow = outflow + jnp.maximum(normal_speed, 0.0)
        inflow = inflow + jnp.minimum(normal_speed, 0.0) * neighbours[side]
    return current + time_step * (
        params[23][None, :] * (gauss - current) - outflow * current - inflow
    )


def per_device(distribution, normals, adjacency, send_list, block_counts):
    vel_local = distribution.shape[0]
    cells = distribution.shape[1]
    total_vel = vel_local * lax.axis_size("vel")
    z_count = total_vel // (VXY * VXY)
    groups = send_list.shape[1]
    slot_count = send_list.shape[2]
    vel_index = lax.axis_index("vel") * vel_local + jnp.arange(vel_local, dtype=jnp.int32)
    velocity = velocity_nodes(vel_index, z_count)
    moment_table = moment_rows(velocity)
    quad_table = quad_rows(velocity).T
    is_local, source, slot_pos = ghost_slots(
        adjacency, block_counts[:, 0], cells, groups, slot_count
    )
    ghost_index = source * slot_count + slot_pos
    local_index = jnp.where(is_local, adjacency, 0)
    send_rows = send_list[0].reshape(-1)

    def reduce_moments(current):
        partial_value = (
            jnp.dot(
                moment_table,
                current,
                precision=lax.Precision.HIGHEST,
                preferred_element_type=jnp.float32,
            )
            / total_vel
        )
        return macroscopic(lax.psum(partial_value, "vel"))

    current = distribution
    for iteration in range(ITERS):
        params = reduce_moments(current)
        ghosts = lax.all_to_all(
            jnp.take(current, send_rows, axis=1), "space", split_axis=1, concat_axis=1, tiled=True
        )
        exponent = jnp.dot(
            quad_table,
            params[13:23],
            precision=lax.Precision.HIGHEST,
            preferred_element_type=jnp.float32,
        )
        equilibrium = jnp.exp(-0.5 * exponent)
        norm_z = lax.psum(jnp.sum(equilibrium, axis=0) / total_vel, "vel")
        neighbours = [
            jnp.where(
                is_local[side][None, :],
                jnp.take(current, local_index[side], axis=1),
                jnp.take(ghosts, ghost_index[side], axis=1),
            )
            for side in range(normals.shape[0])
        ]
        current = relax(current, neighbours, velocity, normals, params, norm_z, equilibrium)
    final = reduce_moments(current)
    return (current, final[:13])


MESH = pl.DeviceIdType.MESH
LOG2E = 1.4426950408889634
QUAD = 4
CHUNKS = 4
PIECES = 8
HELD = 3
HI = lax.Precision.HIGHEST


def coefficient_rows(m):
    full = macroscopic_rows(m)
    scale = -0.5 * LOG2E
    return full[:13], [row * scale for row in full[13:23]], full[23]


def macroscopic_rows(m):
    density = m[0]
    inv_d = 1.0 / density
    ux, uy, uz = (m[1] * inv_d, m[2] * inv_d, m[3] * inv_d)
    b = [m[r] * inv_d for r in range(4, 10)]
    third = [m[r] * inv_d for r in range(10, 13)]
    txx, tyy, tzz = (b[0] - ux * ux, b[1] - uy * uy, b[2] - uz * uz)
    txy, txz, tyz = (b[3] - ux * uy, b[4] - ux * uz, b[5] - uy * uz)
    temper = (txx + tyy + tzz) * (1.0 / 3.0)
    trace_b = b[0] + b[1] + b[2]
    bux = b[0] * ux + b[3] * uy + b[4] * uz
    buy = b[3] * ux + b[1] * uy + b[5] * uz
    buz = b[4] * ux + b[5] * uy + b[2] * uz
    usq = ux * ux + uy * uy + uz * uz
    qx = 0.5 * (third[0] - 2.0 * bux - ux * trace_b + 2.0 * ux * usq)
    qy = 0.5 * (third[1] - 2.0 * buy - uy * trace_b + 2.0 * uy * usq)
    qz = 0.5 * (third[2] - 2.0 * buz - uz * trace_b + 2.0 * uz * usq)
    iso = (1.0 - ellipsoid_mix) * temper
    lxx, lyy, lzz = (iso + ellipsoid_mix * txx, iso + ellipsoid_mix * tyy, iso + ellipsoid_mix * tzz)
    lxy, lxz, lyz = (ellipsoid_mix * txy, ellipsoid_mix * txz, ellipsoid_mix * tyz)
    cxx = lyy * lzz - lyz * lyz
    cxy = lyz * lxz - lxy * lzz
    cxz = lxy * lyz - lyy * lxz
    cyy = lxx * lzz - lxz * lxz
    cyz = lxy * lxz - lxx * lyz
    czz = lxx * lyy - lxy * lxy
    inv_det = 1.0 / (lxx * cxx + lxy * cxy + lxz * cxz)
    ixx, iyy, izz = (cxx * inv_det, cyy * inv_det, czz * inv_det)
    ixy, ixz, iyz = (cxy * inv_det, cxz * inv_det, cyz * inv_det)
    wx = ixx * ux + ixy * uy + ixz * uz
    wy = ixy * ux + iyy * uy + iyz * uz
    wz = ixz * ux + iyz * uy + izz * uz
    offset = ux * wx + uy * wy + uz * wz
    collide = prandtl * density * jnp.exp(visc_power * jnp.log(temper))
    return [
        density, ux, uy, uz, txx, tyy, tzz, txy, txz, tyz, qx, qy, qz,
        ixx, iyy, izz, 2.0 * ixy, 2.0 * ixz, 2.0 * iyz,
        -2.0 * wx, -2.0 * wy, -2.0 * wz, offset, collide,
    ]


def node_velocity(index, z_count):
    shift = VXY.bit_length() - 1
    centre = (VXY - 1) / 2.0
    vx = ((index & (VXY - 1)).astype(jnp.float32) - centre) * spacing
    vy = (((index >> shift) & (VXY - 1)).astype(jnp.float32) - centre) * spacing
    vz = ((index >> (2 * shift)).astype(jnp.float32) - (z_count - 1) / 2.0) * spacing
    return vx, vy, vz


def exponent_at(q, vx, vy, vz):
    return (
        vx * (q[0] * vx + q[3] * vy + q[4] * vz + q[6])
        + vy * (q[1] * vy + q[5] * vz + q[7])
        + (vz * (q[2] * vz + q[8]) + q[9])
    )


def x_column(width):
    rows = lax.broadcasted_iota(jnp.int32, (VXY, width), 0)
    return (rows.astype(jnp.float32) - (VXY - 1) / 2.0) * spacing


def gauss_total(q, width, z_count):
    vx = x_column(width)
    base = (q[0] * vx + q[6]) * vx

    def level(k, acc):
        vz = (k.astype(jnp.float32) - (z_count - 1) / 2.0) * spacing
        slope = q[4] * vz
        odd = q[5] * vz + q[7]
        even = vz * (q[2] * vz + q[8]) + q[9]
        level_base = base + vx * slope + even
        for j in range(VXY // 2):
            vy = (j + 0.5) * spacing
            mid = level_base + q[1] * (vy * vy)
            tilt = (vx * q[3] + odd) * vy
            acc = acc + (jnp.exp2(mid + tilt) + jnp.exp2(mid - tilt))
        return acc

    acc = lax.fori_loop(0, z_count, level, jnp.zeros((VXY, width), jnp.float32))
    return jnp.sum(acc, axis=0, keepdims=True)


def gauss_moments(q, width, z_count):
    vx = x_column(width)
    base = (q[0] * vx + q[6]) * vx
    zero = jnp.zeros((VXY, width), jnp.float32)

    def level(k, carry):
        vz = (k.astype(jnp.float32) - (z_count - 1) / 2.0) * spacing
        slope = q[4] * vz
        odd = q[5] * vz + q[7]
        even = vz * (q[2] * vz + q[8]) + q[9]
        level_base = base + vx * slope + even
        s0, s1, s2, s3 = (zero, zero, zero, zero)
        for j in range(VXY // 2):
            vy = (j + 0.5) * spacing
            mid = level_base + q[1] * (vy * vy)
            tilt = (vx * q[3] + odd) * vy
            up = jnp.exp2(mid + tilt)
            down = jnp.exp2(mid - tilt)
            both = up + down
            diff = (up - down) * vy
            s0 = s0 + both
            s1 = s1 + diff
            s2 = s2 + both * (vy * vy)
            s3 = s3 + diff * (vy * vy)
        z0 = vz * s0
        zz0 = vz * z0
        z1 = vz * s1
        new = (s0, s1, s2, s3, z0, zz0, z1, vz * zz0 + vz * s2, vz * z1)
        return tuple(a + b for a, b in zip(carry, new))

    s0, s1, s2, s3, z0, zz0, z1, zc, zz1 = lax.fori_loop(0, z_count, level, (zero,) * 9)
    vxx = vx * vx
    terms = [
        s0, vx * s0, s1, z0, vxx * s0, s2, zz0, vx * s1, vx * z0, z1,
        vx * (vxx * s0 + s2 + zz0), vxx * s1 + s3 + zz1, vxx * z0 + zc,
    ]
    return [jnp.sum(t, axis=0, keepdims=True) for t in terms]


def split_dot(lhs, rhs):
    return jnp.dot(lhs, rhs, precision=HI, preferred_element_type=jnp.float32)


def step_kernel(
    total_vel,
    f_hbm, n_ref, adj_ref, send_ref,
    out_hbm, fields_ref,
    f_ref, out_ref, load_s, store_s, fx, nx, adjx, sendx, oh, tr0, fnew, tr1, phi_ref,
    qb0, zb0, total_mine, total_theirs, qb1, zb1, qb2, zb2,
    bulk_s, bulk_r, meta_s, meta_r,
    a_s, a_r, b_s, b_r, x_s, x_r,
    d_s, d_r, e_s, e_r, g_s, g_r, h_s, h_r,
):
    nodes, cells = f_hbm.shape
    both = 2 * cells
    faces = n_ref.shape[1]
    z_count = total_vel // (VXY * VXY)
    rows = nodes // CHUNKS
    group = lax.axis_index("space")
    other = 1 - group
    vel = lax.axis_index("vel")
    ring = total_vel // nodes // QUAD
    me_q = lax.rem(vel, QUAD)
    me_z = vel // QUAD

    def at(space, z, q):
        return (space, z * QUAD + q)

    def q_of(step):
        return lax.rem(me_q + step, QUAD)

    def z_of(step):
        return lax.rem(me_z + step, ring)

    barrier = pltpu.get_barrier_semaphore()
    for step in range(1, QUAD):
        pl.semaphore_signal(barrier, inc=1, device_id=at(group, me_z, q_of(step)), device_id_type=MESH)
    for step in range(1, ring):
        pl.semaphore_signal(barrier, inc=1, device_id=at(group, z_of(step), me_q), device_id_type=MESH)
    pl.semaphore_signal(barrier, inc=1, device_id=at(other, me_z, me_q), device_id_type=MESH)

    load = pltpu.make_async_copy(f_hbm, f_ref, load_s)
    load.start()

    lane_v = node_velocity(lax.broadcasted_iota(jnp.int32, (1, nodes), 1) + vel * nodes, z_count)
    lx, ly, lz = lane_v
    sq = lx * lx + ly * ly + lz * lz
    table = [
        jnp.ones_like(lx), lx, ly, lz, lx * lx, ly * ly, lz * lz,
        lx * ly, lx * lz, ly * lz, lx * sq, ly * sq, lz * sq,
    ]
    row_id = lax.broadcasted_iota(jnp.int32, (16, nodes), 0)
    phi = jnp.zeros((16, nodes), jnp.float32)
    for r, row in enumerate(table):
        phi = jnp.where(row_id == r, row, phi)
    phi_ref[...] = phi
    inv_total = 1.0 / total_vel
    load.wait()
    qb0[me_q] = split_dot(phi, f_ref[...]) * inv_total

    pl.semaphore_wait(barrier, QUAD + ring - 1)

    def remote(src, dst, s, r, dev):
        return pltpu.make_async_remote_copy(
            src_ref=src, dst_ref=dst, send_sem=s, recv_sem=r, device_id=dev, device_id_type=MESH
        )

    pair = at(other, me_z, me_q)
    metas = [
        remote(send_ref, sendx, meta_s.at[0], meta_r.at[0], pair),
        remote(adj_ref, adjx, meta_s.at[1], meta_r.at[1], pair),
        remote(n_ref, nx, meta_s.at[2], meta_r.at[2], pair),
    ]
    for copy in metas:
        copy.start()

    def in_quad(buffer, s, r):
        copies = [
            remote(buffer.at[me_q], buffer.at[me_q], s.at[t], r.at[t], at(group, me_z, q_of(t)))
            for t in range(1, QUAD)
        ]
        for copy in copies:
            copy.start()
        return copies

    def along_z(buffer, s, r):
        copies = [
            remote(buffer.at[me_z], buffer.at[me_z], s.at[t], r.at[t], at(group, z_of(t), me_q))
            for t in range(1, ring)
        ]
        for copy in copies:
            copy.start()
        return copies

    def collect(copies, buffer, count):
        for copy in copies:
            copy.wait_recv()
        result = buffer[0]
        for t in range(1, count):
            result = result + buffer[t]
        return result

    piece = nodes // PIECES
    ratio = PIECES // CHUNKS

    def bulk(c):
        part = pl.ds(pl.multiple_of(c * piece, piece), piece)
        return remote(f_ref.at[part], fx.at[part], bulk_s.at[c], bulk_r.at[c], pair)

    first = in_quad(qb0, a_s, a_r)
    for c in range(PIECES - HELD):
        bulk(c).start()

    for copy in metas:
        copy.wait_recv()
    slot_id = lax.broadcasted_iota(jnp.int32, (cells, cells), 0)
    cell_id = lax.broadcasted_iota(jnp.int32, (both, both), 0)

    def listed(send_row, adjacency):
        hit = (slot_id == adjacency - cells).astype(jnp.bfloat16)
        values = jnp.broadcast_to(send_row, (8, cells)).astype(jnp.float32).astype(jnp.bfloat16)
        got = jnp.dot(values, hit, preferred_element_type=jnp.float32)
        return got[0:1].astype(jnp.int32)

    to_me = sendx[0, pl.ds(group, 1), :]
    to_other = send_ref[0, pl.ds(other, 1), :]
    for k in range(faces):
        own = adj_ref[k : k + 1, :]
        theirs = adjx[k : k + 1, :]
        own = jnp.where(own < cells, own, cells + listed(to_me, own))
        theirs = jnp.where(theirs < cells, cells + theirs, listed(to_other, theirs))
        index = jnp.concatenate([own, theirs], axis=1)
        oh[k] = (cell_id == index).astype(jnp.bfloat16)

    zb0[me_z] = collect(first, qb0, QUAD)
    second = along_z(zb0, b_s, b_r)

    def local_velocity(c, width):
        index = lax.broadcasted_iota(jnp.int32, (rows, width), 0) + (vel * nodes + c * rows)
        return node_velocity(index, z_count)

    def transport(state, c, width):
        high = state.astype(jnp.bfloat16)
        low = (state - high.astype(jnp.float32)).astype(jnp.bfloat16)
        lhs = jnp.concatenate([high, low], axis=0)
        vx, vy, vz = local_velocity(c, width)
        mine = state[:, :width]
        result = jnp.zeros((rows, width), jnp.float32)
        for k in range(faces):
            got = jnp.dot(lhs, oh[k, :, 0:width], preferred_element_type=jnp.float32)
            got = got[:rows] + got[rows:]
            normal = []
            for d in range(3):
                line = n_ref[d, k : k + 1, :]
                if width > cells:
                    line = jnp.concatenate([line, nx[d, k : k + 1, :]], axis=1)
                normal.append(line)
            speed = vx * normal[0] + vy * normal[1] + vz * normal[2]
            result = result + (jnp.maximum(speed, 0.0) * mine + jnp.minimum(speed, 0.0) * got)
        return result

    def wide(c):
        part = pl.ds(pl.multiple_of(c * rows, rows), rows)
        return part, jnp.concatenate([f_ref[part, :], fx[part, :]], axis=1)

    def first_transport(c, carry):
        for t in range(ratio):
            bulk(c * ratio + t).wait_recv()
        part, state = wide(c)
        tr0[part, :] = transport(state, c, both)
        return carry

    lax.fori_loop(0, 1, first_transport, 0)
    total_mine[...] = collect(second, zb0, ring)
    third = [remote(total_mine, total_theirs, x_s, x_r, pair)]
    third[0].start()
    for c in range(PIECES - HELD, PIECES):
        bulk(c).start()

    def rows_of(moments):
        return [moments[r : r + 1] for r in range(13)]

    mom0 = rows_of(total_mine[...])
    fields0, own_quad, freq0 = coefficient_rows(mom0)
    sums0 = gauss_moments(own_quad, cells, z_count)
    lift0 = time_step * freq0 * fields0[0] / sums0[0]
    own_gain = lift0 * float(total_vel)
    own_keep = 1.0 - time_step * freq0
    lax.fori_loop(1, CHUNKS - 1, first_transport, 0)
    third[0].wait_recv()
    fields_x, their_quad, freq_x = coefficient_rows(rows_of(total_theirs[...]))
    norm_x = gauss_total(their_quad, cells, z_count) * inv_total
    their_gain = time_step * freq_x * fields_x[0] / norm_x
    their_keep = 1.0 - time_step * freq_x
    quad0 = [jnp.concatenate([a, b], axis=1) for a, b in zip(own_quad, their_quad)]
    gain0 = jnp.concatenate([own_gain, their_gain], axis=1)
    keep0 = jnp.concatenate([own_keep, their_keep], axis=1)
    ahead = nodes - rows
    phi = phi_ref[...]
    m_t0 = split_dot(phi[:, :ahead], tr0[:ahead, :cells])
    lax.fori_loop(CHUNKS - 1, CHUNKS, first_transport, 0)
    qb1[me_q] = (m_t0 + split_dot(phi[:, ahead:], tr0[ahead:, :cells])) * inv_total
    fourth = in_quad(qb1, d_s, d_r)

    def second_transport(c, carry):
        part, state = wide(c)
        vx, vy, vz = local_velocity(c, both)
        state = keep0 * state - time_step * tr0[part, :] + gain0 * jnp.exp2(exponent_at(quad0, vx, vy, vz))
        fnew[part, :] = state[:, :cells]
        tr1[part, :] = transport(state, c, cells)
        return carry

    lax.fori_loop(0, CHUNKS - 1, second_transport, 0)
    zb1[me_z] = collect(fourth, qb1, QUAD)
    sixth = along_z(zb1, g_s, g_r)
    lax.fori_loop(CHUNKS - 1, CHUNKS, second_transport, 0)
    qb2[me_q] = split_dot(phi, tr1[...]) * inv_total
    fifth = in_quad(qb2, e_s, e_r)
    zb2[me_z] = collect(fifth, qb2, QUAD)
    seventh = along_z(zb2, h_s, h_r)
    mom_t0 = collect(sixth, zb1, ring)
    mom1 = [
        own_keep * mom0[r] - time_step * mom_t0[r : r + 1] + lift0 * sums0[r] for r in range(13)
    ]
    fields1, quad1, freq1 = coefficient_rows(mom1)
    sums = gauss_moments(quad1, cells, z_count)
    inv_sum = 1.0 / sums[0]
    lift = time_step * freq1 * fields1[0]
    gain1 = lift * inv_sum * float(total_vel)
    keep1 = 1.0 - time_step * freq1

    def store(c):
        part = pl.ds(pl.multiple_of(c * rows, rows), rows)
        return pltpu.make_async_copy(out_ref.at[part], out_hbm.at[part], store_s.at[c])

    def finish(c, carry):
        part = pl.ds(pl.multiple_of(c * rows, rows), rows)
        vx, vy, vz = local_velocity(c, cells)
        out_ref[part, :] = (
            keep1 * fnew[part, :] - time_step * tr1[part, :]
            + gain1 * jnp.exp2(exponent_at(quad1, vx, vy, vz))
        )
        store(c).start()
        return carry

    lax.fori_loop(0, CHUNKS, finish, 0)
    mom_t = collect(seventh, zb2, ring)
    slope = lift * inv_sum
    last = [
        keep1 * mom1[r] - time_step * mom_t[r : r + 1] + slope * sums[r] for r in range(13)
    ]
    final = macroscopic_rows(last)
    for r in range(13):
        fields_ref[r : r + 1, :] = final[r]
    for c in range(CHUNKS):
        store(c).wait()
    for c in range(PIECES):
        bulk(c).wait_send()
    for copy in metas + first + second + third + fourth + fifth + sixth + seventh:
        copy.wait_send()


def per_device_pair(distribution, normals, adjacency, send_list, block_counts):
    nodes, cells = distribution.shape
    normals = normals.transpose(1, 0, 2)
    size = lax.axis_size("vel")
    ring = size // QUAD
    f32 = jnp.float32
    dma = pltpu.SemaphoreType.DMA
    vmem = pl.BlockSpec(memory_space=pltpu.VMEM)
    anywhere = pl.BlockSpec(memory_space=pl.ANY)
    return pl.pallas_call(
        functools.partial(step_kernel, nodes * size),
        out_shape=(
            jax.ShapeDtypeStruct((nodes, cells), f32),
            jax.ShapeDtypeStruct((13, cells), f32),
        ),
        in_specs=[anywhere] + [vmem] * 3,
        out_specs=(anywhere, vmem),
        scratch_shapes=[
            pltpu.VMEM((nodes, cells), f32),
            pltpu.VMEM((nodes, cells), f32),
            dma,
            dma((CHUNKS,)),
            pltpu.VMEM((nodes, cells), f32),
            pltpu.VMEM(normals.shape, f32),
            pltpu.VMEM(adjacency.shape, jnp.int32),
            pltpu.VMEM(send_list.shape, jnp.int32),
            pltpu.VMEM((normals.shape[1], 2 * cells, 2 * cells), jnp.bfloat16),
            pltpu.VMEM((nodes, 2 * cells), f32),
            pltpu.VMEM((nodes, cells), f32),
            pltpu.VMEM((nodes, cells), f32),
            pltpu.VMEM((16, nodes), f32),
            pltpu.VMEM((QUAD, 16, cells), f32),
            pltpu.VMEM((ring, 16, cells), f32),
            pltpu.VMEM((16, cells), f32),
            pltpu.VMEM((16, cells), f32),
            pltpu.VMEM((QUAD, 16, cells), f32),
            pltpu.VMEM((ring, 16, cells), f32),
            pltpu.VMEM((QUAD, 16, cells), f32),
            pltpu.VMEM((ring, 16, cells), f32),
            dma((PIECES,)), dma((PIECES,)), dma((3,)), dma((3,)),
            dma((QUAD,)), dma((QUAD,)), dma((ring,)), dma((ring,)), dma, dma,
            dma((QUAD,)), dma((QUAD,)), dma((QUAD,)), dma((QUAD,)),
            dma((ring,)), dma((ring,)), dma((ring,)), dma((ring,)),
        ],
        compiler_params=pltpu.CompilerParams(collective_id=0, has_side_effects=True),
        name="steps",
    )(distribution, normals, adjacency, send_list)


def solution(mesh):
    placed = (
        P("vel", "space"),
        P(None, None, "space"),
        P(None, "space"),
        P("space", None, None),
        P(None, "space"),
    )
    pair = mesh.shape["space"] == 2 and mesh.shape["vel"] % QUAD == 0 and ITERS == 2
    return jax.shard_map(
        per_device_pair if pair else per_device,
        mesh=mesh,
        in_specs=placed,
        out_specs=(P("vel", "space"), P(None, "space")),
        check_vma=False,
    )
```

profile of v0, /device:TPU:0, one launch (start us, length us, event | category | flops | bytes accessed | tf_op | source)
XLA Modules:
  0.0 37.0 jit_solution(663749584196880694)
XLA Ops:
  0.6 33.8 %steps.1 = (f32[512,256]{1,0:T(8,128)}, f32[13,256]{1,0:T(8,128)}) custom-call(f32[512,256]{1,0:T(8,128)} %f_hbm.1, f32[3,4,256]{2,1,0:T(4,128)} %bitcast.1, s32[4,256]{1,0:T(4,128)} %adj_ref.1, s32[1,2,256]{2,1,0:T(2,128)} %send_ref.1), custom_call_target="tpu_custom_call" | custom-call | tf_op jit(solution)/shard_map/steps/pallas_call | solution.py:650
  34.5 0.0 copy-start
  34.5 1.9 %copy.8 = f32[512,256]{1,0:T(8,128)} copy(f32[512,256]{1,0:T(8,128)} %get-tuple-element.4) | data formatting | bytes 1048576
  36.4 0.0 copy-done
  36.4 0.6 %copy.9 = f32[13,256]{1,0:T(8,128)} copy(f32[13,256]{1,0:T(8,128)S(1)} %copy-done) | data formatting | bytes 26624
Async XLA Ops:
  34.5 1.9 %copy-start = (f32[13,256]{1,0:T(8,128)S(1)}, f32[13,256]{1,0:T(8,128)}, u32[]{:S(2)}) copy-start(f32[13,256]{1,0:T(8,128)} %get-tuple-element.5) | copy-start | bytes 39940
where the time goes:
time: 37.2 us; the launch traced here: 37 us
  Pallas kernels  33.8 us (91%)
  local copies, waits for them, and re-layouts  2.48 us (7%)
  between operations  0.65 us (2%)
    pallas_call x1, Pallas kernels, per_device_pair(): pl.pallas_call(functools.partial(step_kernel, nodes * size), out_shape=(j...  33.8 us
    unnamed x4, local copies, waits for them, and re-layouts  2.48 us

commit v1 on v0

--- a/solution.py
+++ b/solution.py
@@ -302,76 +302,112 @@
     return vx, vy, vz
 
 
-def exponent_at(q, vx, vy, vz):
-    return (
-        vx * (q[0] * vx + q[3] * vy + q[4] * vz + q[6])
-        + vy * (q[1] * vy + q[5] * vz + q[7])
-        + (vz * (q[2] * vz + q[8]) + q[9])
-    )
-
-
-def x_column(width):
-    rows = lax.broadcasted_iota(jnp.int32, (VXY, width), 0)
-    return (rows.astype(jnp.float32) - (VXY - 1) / 2.0) * spacing
+def x_column(first, rows, width):
+    index = lax.broadcasted_iota(jnp.int32, (rows, width), 0) + first
+    return (index.astype(jnp.float32) - (VXY - 1) / 2.0) * spacing
+
+
+def pair_polynomials(half):
+    def grow(before, now):
+        rows = [now]
+        for _ in range(half - 1):
+            shifted = [0.0] + rows[-1]
+            twice = [2.0 * v for v in rows[-1]] + [0.0]
+            older = before + [0.0] * (len(shifted) - len(before))
+            before = rows[-1]
+            rows.append([x + y - z for x, y, z in zip(shifted, twice, older)])
+        return rows
+
+    return grow([1.0], [1.0]), grow([-1.0], [1.0])
+
+
+def level_coefficients(q, z_count, powers):
+    half = z_count // 2
+    even, odd = pair_polynomials(half)
+    weights = [jnp.exp2(q[2] * ((k + 0.5) * spacing) ** 2) for k in range(half)]
+    result = []
+    for c in range(powers):
+        table = odd if c % 2 else even
+        row = []
+        for j in range(half):
+            total = None
+            for k in range(j, half):
+                term = weights[k] * (table[k][j] * ((k + 0.5) * spacing) ** c)
+                total = term if total is None else total + term
+            row.append(total)
+        result.append(row)
+    return result
+
+
+def horner(row, x):
+    value = row[-1]
+    for c in row[-2::-1]:
+        value = value * x + c
+    return value
+
+
+def gauss_columns(q, width, block):
+    step = 0.5 * spacing
+    vx = x_column(block * 8, 8, width)
+    base = (q[0] * vx + q[6]) * vx + q[9]
+    lean = q[3] * vx + q[7]
+    rise = (q[4] * vx + q[8]) * step
+    for j in range(VXY // 2):
+        vy = (j + 0.5) * spacing
+        mid = base + q[1] * (vy * vy)
+        tilt = lean * vy
+        side = q[5] * (vy * step)
+        columns = []
+        for sign in (1.0, -1.0):
+            flat = jnp.exp2(mid + tilt if sign > 0 else mid - tilt)
+            slope = rise + side if sign > 0 else rise - side
+            up, down = jnp.exp2(slope), jnp.exp2(-slope)
+            diff = up - down
+            columns.append((flat * (up + down), flat * diff, diff * diff))
+        yield vx, vy, columns
 
 
 def gauss_total(q, width, z_count):
-    vx = x_column(width)
-    base = (q[0] * vx + q[6]) * vx
-
-    def level(k, acc):
-        vz = (k.astype(jnp.float32) - (z_count - 1) / 2.0) * spacing
-        slope = q[4] * vz
-        odd = q[5] * vz + q[7]
-        even = vz * (q[2] * vz + q[8]) + q[9]
-        level_base = base + vx * slope + even
-        for j in range(VXY // 2):
-            vy = (j + 0.5) * spacing
-            mid = level_base + q[1] * (vy * vy)
-            tilt = (vx * q[3] + odd) * vy
-            acc = acc + (jnp.exp2(mid + tilt) + jnp.exp2(mid - tilt))
+    (even,) = level_coefficients(q, z_count, 1)
+
+    def block(b, acc):
+        for _, _, columns in gauss_columns(q, width, b):
+            for plus, _, delta in columns:
+                acc = acc + plus * horner(even, delta)
         return acc
 
-    acc = lax.fori_loop(0, z_count, level, jnp.zeros((VXY, width), jnp.float32))
+    acc = lax.fori_loop(0, VXY // 8, block, jnp.zeros((8, width), jnp.float32))
     return jnp.sum(acc, axis=0, keepdims=True)
 
 
 def gauss_moments(q, width, z_count):
-    vx = x_column(width)
-    base = (q[0] * vx + q[6]) * vx
-    zero = jnp.zeros((VXY, width), jnp.float32)
-
-    def level(k, carry):
-        vz = (k.astype(jnp.float32) - (z_count - 1) / 2.0) * spacing
-        slope = q[4] * vz
-        odd = q[5] * vz + q[7]
-        even = vz * (q[2] * vz + q[8]) + q[9]
-        level_base = base + vx * slope + even
-        s0, s1, s2, s3 = (zero, zero, zero, zero)
-        for j in range(VXY // 2):
-            vy = (j + 0.5) * spacing
-            mid = level_base + q[1] * (vy * vy)
-            tilt = (vx * q[3] + odd) * vy
-            up = jnp.exp2(mid + tilt)
-            down = jnp.exp2(mid - tilt)
-            both = up + down
-            diff = (up - down) * vy
-            s0 = s0 + both
-            s1 = s1 + diff
-            s2 = s2 + both * (vy * vy)
-            s3 = s3 + diff * (vy * vy)
-        z0 = vz * s0
-        zz0 = vz * z0
-        z1 = vz * s1
-        new = (s0, s1, s2, s3, z0, zz0, z1, vz * zz0 + vz * s2, vz * z1)
-        return tuple(a + b for a, b in zip(carry, new))
-
-    s0, s1, s2, s3, z0, zz0, z1, zc, zz1 = lax.fori_loop(0, z_count, level, (zero,) * 9)
-    vxx = vx * vx
-    terms = [
-        s0, vx * s0, s1, z0, vxx * s0, s2, zz0, vx * s1, vx * z0, z1,
-        vx * (vxx * s0 + s2 + zz0), vxx * s1 + s3 + zz1, vxx * z0 + zc,
-    ]
+    levels = level_coefficients(q, z_count, 4)
+    zero = jnp.zeros((8, width), jnp.float32)
+
+    def block(b, carry):
+        sums = [[zero] * n for n in (4, 3, 2, 1)]
+        for vx, vy, ((p_up, d_up, x_up), (p_down, d_down, x_down)) in gauss_columns(q, width, b):
+            for c in range(4):
+                above = (d_up if c % 2 else p_up) * horner(levels[c], x_up)
+                below = (d_down if c % 2 else p_down) * horner(levels[c], x_down)
+                both = above + below
+                sums[c][0] = sums[c][0] + both
+                if c < 3:
+                    diff = (above - below) * vy
+                    sums[c][1] = sums[c][1] + diff
+                if c < 2:
+                    sums[c][2] = sums[c][2] + both * (vy * vy)
+                if c < 1:
+                    sums[c][3] = sums[c][3] + diff * (vy * vy)
+        (s0, s1, s2, s3), (z0, z1, z2), (zz0, zz1), (zc,) = sums
+        vxx = vx * vx
+        new = (
+            s0, vx * s0, s1, z0, vxx * s0, s2, zz0, vx * s1, vx * z0, z1,
+            vx * (vxx * s0 + s2 + zz0), vxx * s1 + s3 + zz1, vxx * z0 + z2 + zc,
+        )
+        return tuple(x + y for x, y in zip(carry, new))
+
+    terms = lax.fori_loop(0, VXY // 8, block, (zero,) * 13)
     return [jnp.sum(t, axis=0, keepdims=True) for t in terms]
 
 
@@ -381,17 +417,16 @@
 
 def step_kernel(
     total_vel,
-    f_hbm, n_ref, adj_ref, send_ref,
-    out_hbm, fields_ref,
-    f_ref, out_ref, load_s, store_s, fx, nx, adjx, sendx, oh, tr0, fnew, tr1, phi_ref,
+    f_hbm, n_hbm, adj_hbm, send_hbm,
+    out_ref, fields_ref,
+    f_ref, n_ref, adj_ref, send_ref, load_s,
+    fx, nx, adjx, sendx, ncat, xn, oh, tr0, fnew, tr1, phi_ref,
     qb0, zb0, total_mine, total_theirs, qb1, zb1, qb2, zb2,
-    bulk_s, bulk_r, meta_s, meta_r,
-    a_s, a_r, b_s, b_r, x_s, x_r,
-    d_s, d_r, e_s, e_r, g_s, g_r, h_s, h_r,
+    bulk_s, bulk_r, meta_s, meta_r, stage_s, stage_r,
 ):
     nodes, cells = f_hbm.shape
     both = 2 * cells
-    faces = n_ref.shape[1]
+    faces = n_hbm.shape[1]
     z_count = total_vel // (VXY * VXY)
     rows = nodes // CHUNKS
     group = lax.axis_index("space")
@@ -411,14 +446,25 @@
         return lax.rem(me_z + step, ring)
 
     barrier = pltpu.get_barrier_semaphore()
+    for step in range(1, ring):
+        pl.semaphore_signal(barrier, inc=1, device_id=at(group, z_of(step), me_q), device_id_type=MESH)
     for step in range(1, QUAD):
         pl.semaphore_signal(barrier, inc=1, device_id=at(group, me_z, q_of(step)), device_id_type=MESH)
-    for step in range(1, ring):
-        pl.semaphore_signal(barrier, inc=1, device_id=at(group, z_of(step), me_q), device_id_type=MESH)
     pl.semaphore_signal(barrier, inc=1, device_id=at(other, me_z, me_q), device_id_type=MESH)
 
-    load = pltpu.make_async_copy(f_hbm, f_ref, load_s)
-    load.start()
+    def chunk(c):
+        return pl.ds(pl.multiple_of(c * rows, rows), rows)
+
+    loads = [
+        pltpu.make_async_copy(f_hbm.at[pl.ds(c * rows, rows)], f_ref.at[pl.ds(c * rows, rows)], load_s.at[c])
+        for c in range(CHUNKS)
+    ]
+    small_loads = [
+        pltpu.make_async_copy(src, dst, load_s.at[CHUNKS + i])
+        for i, (src, dst) in enumerate([(send_hbm, send_ref), (adj_hbm, adj_ref), (n_hbm, n_ref)])
+    ]
+    for copy in loads + small_loads:
+        copy.start()
 
     lane_v = node_velocity(lax.broadcasted_iota(jnp.int32, (1, nodes), 1) + vel * nodes, z_count)
     lx, ly, lz = lane_v
@@ -433,10 +479,15 @@
         phi = jnp.where(row_id == r, row, phi)
     phi_ref[...] = phi
     inv_total = 1.0 / total_vel
-    load.wait()
-    qb0[me_q] = split_dot(phi, f_ref[...]) * inv_total
-
-    pl.semaphore_wait(barrier, QUAD + ring - 1)
+    partial = jnp.zeros((16, cells), jnp.float32)
+    for c in range(CHUNKS):
+        loads[c].wait()
+        part = slice(c * rows, (c + 1) * rows)
+        partial = partial + split_dot(phi[:, part], f_ref[part, :])
+    qb0[me_q] = partial * inv_total
+
+    with jax.named_scope("W_bar"):
+        pl.semaphore_wait(barrier, QUAD + ring - 1)
 
     def remote(src, dst, s, r, dev):
         return pltpu.make_async_remote_copy(
@@ -444,35 +495,22 @@
         )
 
     pair = at(other, me_z, me_q)
-    metas = [
-        remote(send_ref, sendx, meta_s.at[0], meta_r.at[0], pair),
-        remote(adj_ref, adjx, meta_s.at[1], meta_r.at[1], pair),
-        remote(n_ref, nx, meta_s.at[2], meta_r.at[2], pair),
-    ]
-    for copy in metas:
-        copy.start()
-
-    def in_quad(buffer, s, r):
-        copies = [
-            remote(buffer.at[me_q], buffer.at[me_q], s.at[t], r.at[t], at(group, me_z, q_of(t)))
-            for t in range(1, QUAD)
-        ]
-        for copy in copies:
-            copy.start()
-        return copies
-
-    def along_z(buffer, s, r):
-        copies = [
-            remote(buffer.at[me_z], buffer.at[me_z], s.at[t], r.at[t], at(group, z_of(t), me_q))
-            for t in range(1, ring)
-        ]
-        for copy in copies:
-            copy.start()
-        return copies
-
-    def collect(copies, buffer, count):
-        for copy in copies:
-            copy.wait_recv()
+
+    def in_quad(buffer, i):
+        for t in range(1, QUAD):
+            remote(buffer.at[me_q], buffer.at[me_q], stage_s.at[i], stage_r.at[i], at(group, me_z, q_of(t))).start()
+
+    def along_z(buffer, i):
+        for t in range(1, ring):
+            remote(buffer.at[me_z], buffer.at[me_z], stage_s.at[i], stage_r.at[i], at(group, z_of(t), me_q)).start()
+
+    def all_of(buffer, sem, count):
+        part = buffer.at[pl.ds(0, count)]
+        pltpu.make_async_copy(part, part, sem).wait()
+
+    def collect(i, buffer, count):
+        with jax.named_scope(f"W_stage{i}"):
+            all_of(buffer, stage_r.at[i], count - 1)
         result = buffer[0]
         for t in range(1, count):
             result = result + buffer[t]
@@ -483,16 +521,35 @@
 
     def bulk(c):
         part = pl.ds(pl.multiple_of(c * piece, piece), piece)
-        return remote(f_ref.at[part], fx.at[part], bulk_s.at[c], bulk_r.at[c], pair)
-
-    first = in_quad(qb0, a_s, a_r)
+        return remote(f_hbm.at[part], fx.at[part], bulk_s, bulk_r.at[c // ratio], pair)
+
+    def bulk_wait(c):
+        with jax.named_scope("W_bulk"):
+            part = fx.at[chunk(c)]
+            pltpu.make_async_copy(part, part, bulk_r.at[c]).wait()
+
+    metas = [
+        remote(send_hbm, sendx, meta_s.at[0], meta_r.at[0], pair),
+        remote(adj_hbm, adjx, meta_s.at[1], meta_r.at[1], pair),
+        remote(n_hbm, nx, meta_s.at[2], meta_r.at[2], pair),
+    ]
+    in_quad(qb0, 0)
+    for copy in metas:
+        copy.start()
     for c in range(PIECES - HELD):
         bulk(c).start()
 
-    for copy in metas:
-        copy.wait_recv()
+    for copy in small_loads:
+        copy.wait()
+    with jax.named_scope("W_meta"):
+        for copy in metas:
+            copy.wait_recv()
+    zb0[me_z] = collect(0, qb0, QUAD)
+    along_z(zb0, 1)
+
     slot_id = lax.broadcasted_iota(jnp.int32, (cells, cells), 0)
     cell_id = lax.broadcasted_iota(jnp.int32, (both, both), 0)
+    diagonal = (cell_id == lax.broadcasted_iota(jnp.int32, (both, both), 1)).astype(jnp.float32)
 
     def listed(send_row, adjacency):
         hit = (slot_id == adjacency - cells).astype(jnp.bfloat16)
@@ -502,56 +559,79 @@
 
     to_me = sendx[0, pl.ds(group, 1), :]
     to_other = send_ref[0, pl.ds(other, 1), :]
+    vx_col = x_column(0, VXY, both)
+    n_sum = [jnp.zeros((1, both), jnp.float32) for _ in range(3)]
     for k in range(faces):
         own = adj_ref[k : k + 1, :]
         theirs = adjx[k : k + 1, :]
         own = jnp.where(own < cells, own, cells + listed(to_me, own))
         theirs = jnp.where(theirs < cells, cells + theirs, listed(to_other, theirs))
         index = jnp.concatenate([own, theirs], axis=1)
-        oh[k] = (cell_id == index).astype(jnp.bfloat16)
-
-    zb0[me_z] = collect(first, qb0, QUAD)
-    second = along_z(zb0, b_s, b_r)
-
-    def local_velocity(c, width):
-        index = lax.broadcasted_iota(jnp.int32, (rows, width), 0) + (vel * nodes + c * rows)
-        return node_velocity(index, z_count)
+        oh[k] = (jnp.where(cell_id == index, 1.0, 0.0) - diagonal).astype(jnp.bfloat16)
+        for d in range(3):
+            line = jnp.concatenate([n_ref[d, k : k + 1, :], nx[d, k : k + 1, :]], axis=1)
+            ncat[d, k : k + 1, :] = line
+            n_sum[d] = n_sum[d] + line
+            if d == 0:
+                xn[k] = vx_col * line
+    for d in range(3):
+        ncat[d, faces : faces + 1, :] = n_sum[d]
+    xn[faces] = vx_col * n_sum[0]
+
+    centre = (VXY - 1) / 2.0
+    shift = VXY.bit_length() - 1
+
+    def line_velocity(c, sub):
+        line = (vel * nodes + c * rows) // VXY + sub
+        vy = ((line & (VXY - 1)).astype(jnp.float32) - centre) * spacing
+        vz = ((line >> shift).astype(jnp.float32) - (z_count - 1) / 2.0) * spacing
+        return vy, vz
+
+    subs = rows // VXY
 
     def transport(state, c, width):
         high = state.astype(jnp.bfloat16)
         low = (state - high.astype(jnp.float32)).astype(jnp.bfloat16)
         lhs = jnp.concatenate([high, low], axis=0)
-        vx, vy, vz = local_velocity(c, width)
-        mine = state[:, :width]
-        result = jnp.zeros((rows, width), jnp.float32)
+        speeds = [line_velocity(c, sub) for sub in range(subs)]
+
+        def speed(k, sub):
+            vy, vz = speeds[sub]
+            return xn[k, :, :width] + (vy * ncat[1, k : k + 1, :width] + vz * ncat[2, k : k + 1, :width])
+
+        result = [state[sub * VXY : (sub + 1) * VXY, :width] * speed(faces, sub) for sub in range(subs)]
         for k in range(faces):
             got = jnp.dot(lhs, oh[k, :, 0:width], preferred_element_type=jnp.float32)
-            got = got[:rows] + got[rows:]
-            normal = []
-            for d in range(3):
-                line = n_ref[d, k : k + 1, :]
-                if width > cells:
-                    line = jnp.concatenate([line, nx[d, k : k + 1, :]], axis=1)
-                normal.append(line)
-            speed = vx * normal[0] + vy * normal[1] + vz * normal[2]
-            result = result + (jnp.maximum(speed, 0.0) * mine + jnp.minimum(speed, 0.0) * got)
-        return result
+            for sub in range(subs):
+                lines = slice(sub * VXY, (sub + 1) * VXY)
+                low_lines = slice(rows + sub * VXY, rows + (sub + 1) * VXY)
+                result[sub] = result[sub] + jnp.minimum(speed(k, sub), 0.0) * (got[lines] + got[low_lines])
+        return jnp.concatenate(result, axis=0)
+
+    def equilibrium(quad, c, width):
+        vx = x_column(0, VXY, width)
+        square = quad[0] * vx
+        parts = []
+        for sub in range(subs):
+            vy, vz = line_velocity(c, sub)
+            slope = quad[3] * vy + quad[4] * vz + quad[6]
+            level = vy * (quad[1] * vy + quad[5] * vz + quad[7]) + (vz * (quad[2] * vz + quad[8]) + quad[9])
+            parts.append(jnp.exp2(vx * (square + slope) + level))
+        return jnp.concatenate(parts, axis=0)
 
     def wide(c):
-        part = pl.ds(pl.multiple_of(c * rows, rows), rows)
+        part = chunk(c)
         return part, jnp.concatenate([f_ref[part, :], fx[part, :]], axis=1)
 
     def first_transport(c, carry):
-        for t in range(ratio):
-            bulk(c * ratio + t).wait_recv()
+        bulk_wait(c)
         part, state = wide(c)
         tr0[part, :] = transport(state, c, both)
         return carry
 
     lax.fori_loop(0, 1, first_transport, 0)
-    total_mine[...] = collect(second, zb0, ring)
-    third = [remote(total_mine, total_theirs, x_s, x_r, pair)]
-    third[0].start()
+    total_mine[...] = collect(1, zb0, ring)
+    remote(total_mine, total_theirs, stage_s.at[2], stage_r.at[2], pair).start()
     for c in range(PIECES - HELD, PIECES):
         bulk(c).start()
 
@@ -560,14 +640,17 @@
 
     mom0 = rows_of(total_mine[...])
     fields0, own_quad, freq0 = coefficient_rows(mom0)
-    sums0 = gauss_moments(own_quad, cells, z_count)
+    with jax.named_scope("G_mom0"):
+        sums0 = gauss_moments(own_quad, cells, z_count)
     lift0 = time_step * freq0 * fields0[0] / sums0[0]
     own_gain = lift0 * float(total_vel)
     own_keep = 1.0 - time_step * freq0
     lax.fori_loop(1, CHUNKS - 1, first_transport, 0)
-    third[0].wait_recv()
+    with jax.named_scope("W_stage2"):
+        pltpu.make_async_copy(total_theirs, total_theirs, stage_r.at[2]).wait()
     fields_x, their_quad, freq_x = coefficient_rows(rows_of(total_theirs[...]))
-    norm_x = gauss_total(their_quad, cells, z_count) * inv_total
+    with jax.named_scope("G_tot"):
+        norm_x = gauss_total(their_quad, cells, z_count) * inv_total
     their_gain = time_step * freq_x * fields_x[0] / norm_x
     their_keep = 1.0 - time_step * freq_x
     quad0 = [jnp.concatenate([a, b], axis=1) for a, b in zip(own_quad, their_quad)]
@@ -578,51 +661,44 @@
     m_t0 = split_dot(phi[:, :ahead], tr0[:ahead, :cells])
     lax.fori_loop(CHUNKS - 1, CHUNKS, first_transport, 0)
     qb1[me_q] = (m_t0 + split_dot(phi[:, ahead:], tr0[ahead:, :cells])) * inv_total
-    fourth = in_quad(qb1, d_s, d_r)
+    in_quad(qb1, 3)
 
     def second_transport(c, carry):
         part, state = wide(c)
-        vx, vy, vz = local_velocity(c, both)
-        state = keep0 * state - time_step * tr0[part, :] + gain0 * jnp.exp2(exponent_at(quad0, vx, vy, vz))
+        state = keep0 * state - time_step * tr0[part, :] + gain0 * equilibrium(quad0, c, both)
         fnew[part, :] = state[:, :cells]
         tr1[part, :] = transport(state, c, cells)
         return carry
 
     lax.fori_loop(0, CHUNKS - 1, second_transport, 0)
-    zb1[me_z] = collect(fourth, qb1, QUAD)
-    sixth = along_z(zb1, g_s, g_r)
+    zb1[me_z] = collect(3, qb1, QUAD)
+    along_z(zb1, 4)
     lax.fori_loop(CHUNKS - 1, CHUNKS, second_transport, 0)
     qb2[me_q] = split_dot(phi, tr1[...]) * inv_total
-    fifth = in_quad(qb2, e_s, e_r)
-    zb2[me_z] = collect(fifth, qb2, QUAD)
-    seventh = along_z(zb2, h_s, h_r)
-    mom_t0 = collect(sixth, zb1, ring)
+    in_quad(qb2, 5)
+    zb2[me_z] = collect(5, qb2, QUAD)
+    along_z(zb2, 6)
+    mom_t0 = collect(4, zb1, ring)
     mom1 = [
         own_keep * mom0[r] - time_step * mom_t0[r : r + 1] + lift0 * sums0[r] for r in range(13)
     ]
     fields1, quad1, freq1 = coefficient_rows(mom1)
-    sums = gauss_moments(quad1, cells, z_count)
+    with jax.named_scope("G_mom1"):
+        sums = gauss_moments(quad1, cells, z_count)
     inv_sum = 1.0 / sums[0]
     lift = time_step * freq1 * fields1[0]
     gain1 = lift * inv_sum * float(total_vel)
     keep1 = 1.0 - time_step * freq1
 
-    def store(c):
-        part = pl.ds(pl.multiple_of(c * rows, rows), rows)
-        return pltpu.make_async_copy(out_ref.at[part], out_hbm.at[part], store_s.at[c])
-
     def finish(c, carry):
-        part = pl.ds(pl.multiple_of(c * rows, rows), rows)
-        vx, vy, vz = local_velocity(c, cells)
+        part = chunk(c)
         out_ref[part, :] = (
-            keep1 * fnew[part, :] - time_step * tr1[part, :]
-            + gain1 * jnp.exp2(exponent_at(quad1, vx, vy, vz))
+            keep1 * fnew[part, :] - time_step * tr1[part, :] + gain1 * equilibrium(quad1, c, cells)
         )
-        store(c).start()
         return carry
 
     lax.fori_loop(0, CHUNKS, finish, 0)
-    mom_t = collect(seventh, zb2, ring)
+    mom_t = collect(6, zb2, ring)
     slope = lift * inv_sum
     last = [
         keep1 * mom1[r] - time_step * mom_t[r : r + 1] + slope * sums[r] for r in range(13)
@@ -630,12 +706,28 @@
     final = macroscopic_rows(last)
     for r in range(13):
         fields_ref[r : r + 1, :] = final[r]
-    for c in range(CHUNKS):
-        store(c).wait()
-    for c in range(PIECES):
-        bulk(c).wait_send()
-    for copy in metas + first + second + third + fourth + fifth + sixth + seventh:
-        copy.wait_send()
+    with jax.named_scope("W_send"):
+        pltpu.make_async_copy(fx, fx, bulk_s).wait()
+        for copy in metas:
+            copy.wait_send()
+        for i, (buffer, count) in enumerate([
+            (qb0, QUAD - 1), (zb0, ring - 1), (None, 0), (qb1, QUAD - 1), (zb1, ring - 1), (qb2, QUAD - 1), (zb2, ring - 1),
+        ]):
+            if buffer is None:
+                pltpu.make_async_copy(total_mine, total_mine, stage_s.at[i]).wait()
+            else:
+                all_of(buffer, stage_s.at[i], count)
+
+
+def store_kernel(state_ref, fields_ref, state_out, fields_out, sems):
+    copies = [
+        pltpu.make_async_copy(fields_ref, fields_out, sems.at[0]),
+        pltpu.make_async_copy(state_ref, state_out, sems.at[1]),
+    ]
+    for copy in copies:
+        copy.start()
+    for copy in copies:
+        copy.wait()
 
 
 def per_device_pair(distribution, normals, adjacency, send_list, block_counts):
@@ -643,28 +735,33 @@
     normals = normals.transpose(1, 0, 2)
     size = lax.axis_size("vel")
     ring = size // QUAD
+    faces = normals.shape[1]
     f32 = jnp.float32
     dma = pltpu.SemaphoreType.DMA
     vmem = pl.BlockSpec(memory_space=pltpu.VMEM)
-    anywhere = pl.BlockSpec(memory_space=pl.ANY)
-    return pl.pallas_call(
+    hbm = pl.BlockSpec(memory_space=pltpu.HBM)
+    shapes = (
+        jax.ShapeDtypeStruct((nodes, cells), f32),
+        jax.ShapeDtypeStruct((13, cells), f32),
+    )
+    state, fields = pl.pallas_call(
         functools.partial(step_kernel, nodes * size),
-        out_shape=(
-            jax.ShapeDtypeStruct((nodes, cells), f32),
-            jax.ShapeDtypeStruct((13, cells), f32),
-        ),
-        in_specs=[anywhere] + [vmem] * 3,
-        out_specs=(anywhere, vmem),
+        out_shape=shapes,
+        in_specs=[hbm] * 4,
+        out_specs=(vmem, vmem),
         scratch_shapes=[
-            pltpu.VMEM((nodes, cells), f32),
-            pltpu.VMEM((nodes, cells), f32),
-            dma,
-            dma((CHUNKS,)),
             pltpu.VMEM((nodes, cells), f32),
             pltpu.VMEM(normals.shape, f32),
             pltpu.VMEM(adjacency.shape, jnp.int32),
             pltpu.VMEM(send_list.shape, jnp.int32),
-            pltpu.VMEM((normals.shape[1], 2 * cells, 2 * cells), jnp.bfloat16),
+            dma((CHUNKS + 3,)),
+            pltpu.VMEM((nodes, cells), f32),
+            pltpu.VMEM(normals.shape, f32),
+            pltpu.VMEM(adjacency.shape, jnp.int32),
+            pltpu.VMEM(send_list.shape, jnp.int32),
+            pltpu.VMEM((3, 8, 2 * cells), f32),
+            pltpu.VMEM((faces + 1, VXY, 2 * cells), f32),
+            pltpu.VMEM((faces, 2 * cells, 2 * cells), jnp.bfloat16),
             pltpu.VMEM((nodes, 2 * cells), f32),
             pltpu.VMEM((nodes, cells), f32),
             pltpu.VMEM((nodes, cells), f32),
@@ -677,14 +774,23 @@
             pltpu.VMEM((ring, 16, cells), f32),
             pltpu.VMEM((QUAD, 16, cells), f32),
             pltpu.VMEM((ring, 16, cells), f32),
-            dma((PIECES,)), dma((PIECES,)), dma((3,)), dma((3,)),
-            dma((QUAD,)), dma((QUAD,)), dma((ring,)), dma((ring,)), dma, dma,
-            dma((QUAD,)), dma((QUAD,)), dma((QUAD,)), dma((QUAD,)),
-            dma((ring,)), dma((ring,)), dma((ring,)), dma((ring,)),
+            dma, dma((CHUNKS,)), dma((3,)), dma((3,)), dma((7,)), dma((7,)),
         ],
-        compiler_params=pltpu.CompilerParams(collective_id=0, has_side_effects=True),
+        compiler_params=pltpu.CompilerParams(
+            collective_id=0, has_side_effects=True, vmem_limit_bytes=16 * 1024 * 1024
+        ),
         name="steps",
-    )(distribution, normals, adjacency, send_list)
+    )(*[pltpu.with_memory_space_constraint(x, pltpu.HBM) for x in (distribution, normals, adjacency, send_list)])
+    anywhere = pl.BlockSpec(memory_space=pl.ANY)
+    return pl.pallas_call(
+        store_kernel,
+        out_shape=shapes,
+        in_specs=[anywhere, anywhere],
+        out_specs=(hbm, hbm),
+        scratch_shapes=[dma((2,))],
+        compiler_params=pltpu.CompilerParams(vmem_limit_bytes=16 * 1024 * 1024),
+        name="store",
+    )(state, fields)
 
 
 def solution(mesh):

time: 37.2 us -> 32.7 us (0.88)
  local copies, waits for them, and re-layouts: 2.48 us -> 0 us
  Pallas kernels: 33.8 us -> 31.9 us
    unnamed x4 -> x0, local copies, waits for them, and re-layouts: 2.48 us -> none
    pallas_call x1 -> x2, Pallas kernels: 33.8 us -> 31.9 us  [the longest x1 31.1 us: per_device_pair(): pl.pallas_call(functools.partial(step_kernel, nodes * size), out_shape=sh...]
where the time goes in v1:
time: 32.7 us; the launch traced here: 32.5 us
  Pallas kernels  31.9 us (98%)
  between operations  0.64 us (2%)
    pallas_call x1, Pallas kernels, per_device_pair(): pl.pallas_call(functools.partial(step_kernel, nodes * size), out_shape=sh...  31.1 us
    pallas_call x1, Pallas kernels, per_device_pair(): pl.pallas_call(store_kernel, out_shape=shapes, in_specs=[anywhere, anywhe...  0.82 us

profile of v1, /device:TPU:0, one launch (start us, length us, event | category | flops | bytes accessed | tf_op | source)
XLA Modules:
  0.0 32.5 jit_solution(2459404238488995259)
XLA Ops:
  0.6 31.1 %steps.1 = (f32[512,256]{1,0:T(8,128)S(1)}, f32[13,256]{1,0:T(8,128)S(1)}) custom-call(f32[512,256]{1,0:T(8,128)} %f_hbm.1, f32[3,4,256]{2,1,0:T(4,128)} %bitcast.1, s32[4,256]{1,0:T(4,128)} %adj_hbm.1, s32[1,2,256]{2,1,0:T(2,128)} %send_hbm.1), custom_call_target="tpu_custom_call" | custom-call | tf_op jit(solution)/shard_map/steps/pallas_call | solution.py:747
  31.7 0.8 %store.1 = (f32[512,256]{1,0:T(8,128)}, f32[13,256]{1,0:T(8,128)}) custom-call(f32[512,256]{1,0:T(8,128)S(1)} %get-tuple-element.4.state_ref, f32[13,256]{1,0:T(8,128)S(1)} %get-tuple-element.5.fields_ref), custom_call_target="tpu_custom_call" | custom-call | tf_op jit(solution)/shard_map/store/pallas_call | solution.py:785

commit v2 on v1

--- a/solution.py
+++ b/solution.py
@@ -241,8 +241,10 @@
 LOG2E = 1.4426950408889634
 QUAD = 4
 CHUNKS = 4
-PIECES = 8
-HELD = 3
+PIECES = 16
+MARKS = (5, 8, 11)
+SLABS = 2
+EARLY = 3
 HI = lax.Precision.HIGHEST
 
 
@@ -420,8 +422,8 @@
     f_hbm, n_hbm, adj_hbm, send_hbm,
     out_ref, fields_ref,
     f_ref, n_ref, adj_ref, send_ref, load_s,
-    fx, nx, adjx, sendx, ncat, xn, oh, tr0, fnew, tr1, phi_ref,
-    qb0, zb0, total_mine, total_theirs, qb1, zb1, qb2, zb2,
+    fx, nx, adjx, sendx, ncat, xn, oh, tr0, wide, fnew, tr1, phi_ref, phi_two,
+    qb0, zb0, total_mine, total_theirs, qb1, zb1, qb2, zb2, lent0, got0, lent1, got1,
     bulk_s, bulk_r, meta_s, meta_r, stage_s, stage_r,
 ):
     nodes, cells = f_hbm.shape
@@ -478,6 +480,9 @@
     for r, row in enumerate(table):
         phi = jnp.where(row_id == r, row, phi)
     phi_ref[...] = phi
+    phi_high = phi.astype(jnp.bfloat16)
+    phi_two[0:16, :] = phi_high
+    phi_two[16:32, :] = (phi - phi_high.astype(jnp.float32)).astype(jnp.bfloat16)
     inv_total = 1.0 / total_vel
     partial = jnp.zeros((16, cells), jnp.float32)
     for c in range(CHUNKS):
@@ -504,6 +509,13 @@
         for t in range(1, ring):
             remote(buffer.at[me_z], buffer.at[me_z], stage_s.at[i], stage_r.at[i], at(group, z_of(t), me_q)).start()
 
+    def across(src, dst, i):
+        remote(src, dst, stage_s.at[i], stage_r.at[i], pair).start()
+
+    def arrived(dst, i):
+        with jax.named_scope(f"W_stage{i}"):
+            pltpu.make_async_copy(dst, dst, stage_r.at[i]).wait()
+
     def all_of(buffer, sem, count):
         part = buffer.at[pl.ds(0, count)]
         pltpu.make_async_copy(part, part, sem).wait()
@@ -519,9 +531,10 @@
     piece = nodes // PIECES
     ratio = PIECES // CHUNKS
 
-    def bulk(c):
-        part = pl.ds(pl.multiple_of(c * piece, piece), piece)
-        return remote(f_hbm.at[part], fx.at[part], bulk_s, bulk_r.at[c // ratio], pair)
+    def bulk(first, last):
+        for c in range(first, last):
+            part = pl.ds(c * piece, piece)
+            remote(f_hbm.at[part], fx.at[part], bulk_s, bulk_r.at[c // ratio], pair).start()
 
     def bulk_wait(c):
         with jax.named_scope("W_bulk"):
@@ -536,152 +549,203 @@
     in_quad(qb0, 0)
     for copy in metas:
         copy.start()
-    for c in range(PIECES - HELD):
-        bulk(c).start()
+    bulk(0, MARKS[0])
 
     for copy in small_loads:
         copy.wait()
+    mine, far = slice(0, cells), slice(cells, both)
+    slot_id = lax.broadcasted_iota(jnp.int32, (cells, cells), 0)
+    eye = (slot_id == lax.broadcasted_iota(jnp.int32, (cells, cells), 1)).astype(jnp.float32)
+    vx_col = x_column(0, VXY, cells)
+
+    def listed(send_row, adjacency):
+        hit = jnp.where(slot_id == adjacency - cells, 1.0, 0.0).astype(jnp.bfloat16)
+        values = jnp.broadcast_to(send_row, (8, cells)).astype(jnp.float32).astype(jnp.bfloat16)
+        got = jnp.dot(values, hit, preferred_element_type=jnp.float32)
+        return jnp.where(adjacency < cells, -1, got[0:1].astype(jnp.int32))
+
+    def choose(k, source, target, index):
+        hit = jnp.where(slot_id == index, 1.0, 0.0)
+        oh[k, source, target] = (hit - eye if source == target else hit).astype(jnp.bfloat16)
+
+    def lay_normals(ref, target):
+        for d in range(3):
+            lines = [ref[d, k : k + 1, :] for k in range(faces)]
+            lines.append(sum(lines[1:], lines[0]))
+            for k, line in enumerate(lines):
+                if d == 0:
+                    xn[k, :, target] = vx_col * line
+                else:
+                    ncat[d, k : k + 1, target] = line
+
+    lay_normals(n_ref, mine)
+    for k in range(faces):
+        choose(k, mine, mine, adj_ref[k : k + 1, :])
+
+    zb0[me_z] = collect(0, qb0, QUAD)
+    along_z(zb0, 1)
+
     with jax.named_scope("W_meta"):
         for copy in metas:
             copy.wait_recv()
-    zb0[me_z] = collect(0, qb0, QUAD)
-    along_z(zb0, 1)
-
-    slot_id = lax.broadcasted_iota(jnp.int32, (cells, cells), 0)
-    cell_id = lax.broadcasted_iota(jnp.int32, (both, both), 0)
-    diagonal = (cell_id == lax.broadcasted_iota(jnp.int32, (both, both), 1)).astype(jnp.float32)
-
-    def listed(send_row, adjacency):
-        hit = (slot_id == adjacency - cells).astype(jnp.bfloat16)
-        values = jnp.broadcast_to(send_row, (8, cells)).astype(jnp.float32).astype(jnp.bfloat16)
-        got = jnp.dot(values, hit, preferred_element_type=jnp.float32)
-        return got[0:1].astype(jnp.int32)
-
     to_me = sendx[0, pl.ds(group, 1), :]
     to_other = send_ref[0, pl.ds(other, 1), :]
-    vx_col = x_column(0, VXY, both)
-    n_sum = [jnp.zeros((1, both), jnp.float32) for _ in range(3)]
+    lay_normals(nx, far)
     for k in range(faces):
-        own = adj_ref[k : k + 1, :]
-        theirs = adjx[k : k + 1, :]
-        own = jnp.where(own < cells, own, cells + listed(to_me, own))
-        theirs = jnp.where(theirs < cells, cells + theirs, listed(to_other, theirs))
-        index = jnp.concatenate([own, theirs], axis=1)
-        oh[k] = (jnp.where(cell_id == index, 1.0, 0.0) - diagonal).astype(jnp.bfloat16)
-        for d in range(3):
-            line = jnp.concatenate([n_ref[d, k : k + 1, :], nx[d, k : k + 1, :]], axis=1)
-            ncat[d, k : k + 1, :] = line
-            n_sum[d] = n_sum[d] + line
-            if d == 0:
-                xn[k] = vx_col * line
-    for d in range(3):
-        ncat[d, faces : faces + 1, :] = n_sum[d]
-    xn[faces] = vx_col * n_sum[0]
+        choose(k, mine, far, listed(to_other, adjx[k : k + 1, :]))
 
     centre = (VXY - 1) / 2.0
     shift = VXY.bit_length() - 1
 
-    def line_velocity(c, sub):
-        line = (vel * nodes + c * rows) // VXY + sub
+    def line_velocity(first):
+        line = (vel * nodes + first) // VXY
         vy = ((line & (VXY - 1)).astype(jnp.float32) - centre) * spacing
         vz = ((line >> shift).astype(jnp.float32) - (z_count - 1) / 2.0) * spacing
         return vy, vz
 
-    subs = rows // VXY
-
-    def transport(state, c, width):
+    def halves(state):
         high = state.astype(jnp.bfloat16)
         low = (state - high.astype(jnp.float32)).astype(jnp.bfloat16)
-        lhs = jnp.concatenate([high, low], axis=0)
-        speeds = [line_velocity(c, sub) for sub in range(subs)]
+        return jnp.concatenate([high, low], axis=0)
+
+    def transport(lhs, source, target, leaving, first, count):
+        speeds = [line_velocity(first + sub * VXY) for sub in range(count // VXY)]
 
         def speed(k, sub):
             vy, vz = speeds[sub]
-            return xn[k, :, :width] + (vy * ncat[1, k : k + 1, :width] + vz * ncat[2, k : k + 1, :width])
-
-        result = [state[sub * VXY : (sub + 1) * VXY, :width] * speed(faces, sub) for sub in range(subs)]
+            return xn[k, :, target] + (vy * ncat[1, k : k + 1, target] + vz * ncat[2, k : k + 1, target])
+
+        def lines(sub, offset=0):
+            return slice(offset + sub * VXY, offset + (sub + 1) * VXY)
+
+        result = [
+            None if leaving is None else leaving[lines(sub)] * speed(faces, sub) for sub in range(count // VXY)
+        ]
         for k in range(faces):
-            got = jnp.dot(lhs, oh[k, :, 0:width], preferred_element_type=jnp.float32)
-            for sub in range(subs):
-                lines = slice(sub * VXY, (sub + 1) * VXY)
-                low_lines = slice(rows + sub * VXY, rows + (sub + 1) * VXY)
-                result[sub] = result[sub] + jnp.minimum(speed(k, sub), 0.0) * (got[lines] + got[low_lines])
+            got = jnp.dot(lhs, oh[k, source, target], preferred_element_type=jnp.float32)
+            for sub in range(count // VXY):
+                value = got[lines(sub)]
+                if lhs.shape[0] > count:
+                    value = value + got[lines(sub, count)]
+                term = jnp.minimum(speed(k, sub), 0.0) * value
+                result[sub] = term if result[sub] is None else result[sub] + term
         return jnp.concatenate(result, axis=0)
 
-    def equilibrium(quad, c, width):
-        vx = x_column(0, VXY, width)
-        square = quad[0] * vx
+    def equilibrium(quad, first, count):
+        square = quad[0] * vx_col
         parts = []
-        for sub in range(subs):
-            vy, vz = line_velocity(c, sub)
+        for sub in range(count // VXY):
+            vy, vz = line_velocity(first + sub * VXY)
             slope = quad[3] * vy + quad[4] * vz + quad[6]
             level = vy * (quad[1] * vy + quad[5] * vz + quad[7]) + (vz * (quad[2] * vz + quad[8]) + quad[9])
-            parts.append(jnp.exp2(vx * (square + slope) + level))
+            parts.append(jnp.exp2(vx_col * (square + slope) + level))
         return jnp.concatenate(parts, axis=0)
 
-    def wide(c):
-        part = chunk(c)
-        return part, jnp.concatenate([f_ref[part, :], fx[part, :]], axis=1)
-
-    def first_transport(c, carry):
-        bulk_wait(c)
-        part, state = wide(c)
-        tr0[part, :] = transport(state, c, both)
-        return carry
-
-    lax.fori_loop(0, 1, first_transport, 0)
+    def two_dot(part, state):
+        high = state.astype(jnp.bfloat16)
+        low = (state - high.astype(jnp.float32)).astype(jnp.bfloat16)
+        first = jnp.dot(phi_two[:, part], high, preferred_element_type=jnp.float32)
+        return first[0:16] + first[16:32] + jnp.dot(phi_two[0:16, part], low, preferred_element_type=jnp.float32)
+
+    blocks = [(c * (nodes // SLABS), nodes // SLABS) for c in range(SLABS)]
+    sent = jnp.zeros((16, cells), jnp.float32)
+    with jax.named_scope("T0p"):
+        for first, count in blocks:
+            part = slice(first, first + count)
+            state = f_ref[part, :]
+            lhs = halves(state)
+            tr0[part, mine] = transport(lhs, mine, mine, state, first, count)
+            moved = transport(lhs, mine, far, None, first, count)
+            tr0[part, far] = moved
+            sent = sent + two_dot(part, moved)
+    lent0[...] = sent * (-time_step * inv_total)
+    across(lent0, got0, 7)
+    bulk(MARKS[0], MARKS[1])
+
+    with jax.named_scope("oh2"):
+        for k in range(faces):
+            choose(k, far, mine, listed(to_me, adj_ref[k : k + 1, :]))
+            theirs = adjx[k : k + 1, :]
+            choose(k, far, far, theirs)
+
     total_mine[...] = collect(1, zb0, ring)
-    remote(total_mine, total_theirs, stage_s.at[2], stage_r.at[2], pair).start()
-    for c in range(PIECES - HELD, PIECES):
-        bulk(c).start()
+    across(total_mine, total_theirs, 2)
+    bulk(MARKS[1], MARKS[2])
 
     def rows_of(moments):
         return [moments[r : r + 1] for r in range(13)]
 
-    mom0 = rows_of(total_mine[...])
-    fields0, own_quad, freq0 = coefficient_rows(mom0)
-    with jax.named_scope("G_mom0"):
-        sums0 = gauss_moments(own_quad, cells, z_count)
-    lift0 = time_step * freq0 * fields0[0] / sums0[0]
-    own_gain = lift0 * float(total_vel)
+    fields0, own_quad, freq0 = coefficient_rows(rows_of(total_mine[...]))
+    with jax.named_scope("G_tot0"):
+        norm0 = gauss_total(own_quad, cells, z_count) * inv_total
+    own_gain = time_step * freq0 * fields0[0] / norm0
     own_keep = 1.0 - time_step * freq0
-    lax.fori_loop(1, CHUNKS - 1, first_transport, 0)
-    with jax.named_scope("W_stage2"):
-        pltpu.make_async_copy(total_theirs, total_theirs, stage_r.at[2]).wait()
+
+    with jax.named_scope("f1p"):
+        for first, count in blocks:
+            part = slice(first, first + count)
+            state = (
+                own_keep * f_ref[part, :] - time_step * tr0[part, mine] + own_gain * equilibrium(own_quad, first, count)
+            )
+            fnew[part, :] = state
+            wide[part, mine] = state.astype(jnp.bfloat16)
+            away = -time_step * tr0[part, far]
+            tr0[part, far] = away
+            wide[part, far] = away.astype(jnp.bfloat16)
+        kept = split_dot(phi_ref[...], fnew[...]) * inv_total
+    arrived(got0, 7)
+    qb1[me_q] = kept + got0[...]
+    in_quad(qb1, 3)
+
+    def second_moments(target, leaving):
+        total = jnp.zeros((16, cells), jnp.float32)
+        for first, count in blocks:
+            part = slice(first, first + count)
+            moved = transport(wide[part, :], slice(0, both), target, leaving(part), first, count)
+            total = total + two_dot(part, moved)
+        return total * inv_total
+
+    with jax.named_scope("T1p_far"):
+        lent1[...] = second_moments(far, lambda part: tr0[part, far])
+    across(lent1, got1, 8)
+    bulk(MARKS[2], PIECES)
+    with jax.named_scope("T1p_mine"):
+        stay = second_moments(mine, lambda part: fnew[part, :])
+
+    zb1[me_z] = collect(3, qb1, QUAD)
+    along_z(zb1, 4)
+
+    arrived(total_theirs, 2)
     fields_x, their_quad, freq_x = coefficient_rows(rows_of(total_theirs[...]))
-    with jax.named_scope("G_tot"):
+    with jax.named_scope("G_totx"):
         norm_x = gauss_total(their_quad, cells, z_count) * inv_total
     their_gain = time_step * freq_x * fields_x[0] / norm_x
     their_keep = 1.0 - time_step * freq_x
-    quad0 = [jnp.concatenate([a, b], axis=1) for a, b in zip(own_quad, their_quad)]
-    gain0 = jnp.concatenate([own_gain, their_gain], axis=1)
-    keep0 = jnp.concatenate([own_keep, their_keep], axis=1)
-    ahead = nodes - rows
-    phi = phi_ref[...]
-    m_t0 = split_dot(phi[:, :ahead], tr0[:ahead, :cells])
-    lax.fori_loop(CHUNKS - 1, CHUNKS, first_transport, 0)
-    qb1[me_q] = (m_t0 + split_dot(phi[:, ahead:], tr0[ahead:, :cells])) * inv_total
-    in_quad(qb1, 3)
-
-    def second_transport(c, carry):
-        part, state = wide(c)
-        state = keep0 * state - time_step * tr0[part, :] + gain0 * equilibrium(quad0, c, both)
-        fnew[part, :] = state[:, :cells]
-        tr1[part, :] = transport(state, c, cells)
+
+    arrived(got1, 8)
+    qb2[me_q] = stay + got1[...]
+    in_quad(qb2, 5)
+
+    def received(c, carry):
+        bulk_wait(c)
+        part, first = chunk(c), c * rows
+        state = fx[part, :]
+        lhs = halves(state)
+        here = fnew[part, :] - time_step * transport(lhs, far, mine, None, first, rows)
+        there = (
+            their_keep * state
+            + (tr0[part, far] - time_step * transport(lhs, far, far, state, first, rows))
+            + their_gain * equilibrium(their_quad, first, rows)
+        )
+        fnew[part, :] = here
+        lhs = halves(jnp.concatenate([here, there], axis=1))
+        tr1[part, :] = transport(lhs, slice(0, both), mine, here, first, rows)
         return carry
 
-    lax.fori_loop(0, CHUNKS - 1, second_transport, 0)
-    zb1[me_z] = collect(3, qb1, QUAD)
-    along_z(zb1, 4)
-    lax.fori_loop(CHUNKS - 1, CHUNKS, second_transport, 0)
-    qb2[me_q] = split_dot(phi, tr1[...]) * inv_total
-    in_quad(qb2, 5)
+    lax.fori_loop(0, EARLY, received, 0)
     zb2[me_z] = collect(5, qb2, QUAD)
     along_z(zb2, 6)
-    mom_t0 = collect(4, zb1, ring)
-    mom1 = [
-        own_keep * mom0[r] - time_step * mom_t0[r : r + 1] + lift0 * sums0[r] for r in range(13)
-    ]
+    mom1 = rows_of(collect(4, zb1, ring))
     fields1, quad1, freq1 = coefficient_rows(mom1)
     with jax.named_scope("G_mom1"):
         sums = gauss_moments(quad1, cells, z_count)
@@ -689,15 +753,17 @@
     lift = time_step * freq1 * fields1[0]
     gain1 = lift * inv_sum * float(total_vel)
     keep1 = 1.0 - time_step * freq1
+    lax.fori_loop(EARLY, CHUNKS, received, 0)
 
     def finish(c, carry):
         part = chunk(c)
         out_ref[part, :] = (
-            keep1 * fnew[part, :] - time_step * tr1[part, :] + gain1 * equilibrium(quad1, c, cells)
+            keep1 * fnew[part, :] - time_step * tr1[part, :] + gain1 * equilibrium(quad1, c * rows, rows)
         )
         return carry
 
-    lax.fori_loop(0, CHUNKS, finish, 0)
+    with jax.named_scope("fin"):
+        lax.fori_loop(0, CHUNKS, finish, 0)
     mom_t = collect(6, zb2, ring)
     slope = lift * inv_sum
     last = [
@@ -710,13 +776,12 @@
         pltpu.make_async_copy(fx, fx, bulk_s).wait()
         for copy in metas:
             copy.wait_send()
-        for i, (buffer, count) in enumerate([
-            (qb0, QUAD - 1), (zb0, ring - 1), (None, 0), (qb1, QUAD - 1), (zb1, ring - 1), (qb2, QUAD - 1), (zb2, ring - 1),
-        ]):
-            if buffer is None:
-                pltpu.make_async_copy(total_mine, total_mine, stage_s.at[i]).wait()
-            else:
-                all_of(buffer, stage_s.at[i], count)
+        for i, buffer in ((2, total_mine), (7, lent0), (8, lent1)):
+            pltpu.make_async_copy(buffer, buffer, stage_s.at[i]).wait()
+        for i, buffer, count in (
+            (0, qb0, QUAD), (1, zb0, ring), (3, qb1, QUAD), (4, zb1, ring), (5, qb2, QUAD), (6, zb2, ring),
+        ):
+            all_of(buffer, stage_s.at[i], count - 1)
 
 
 def store_kernel(state_ref, fields_ref, state_out, fields_out, sems):
@@ -763,9 +828,11 @@
             pltpu.VMEM((faces + 1, VXY, 2 * cells), f32),
             pltpu.VMEM((faces, 2 * cells, 2 * cells), jnp.bfloat16),
             pltpu.VMEM((nodes, 2 * cells), f32),
+            pltpu.VMEM((nodes, 2 * cells), jnp.bfloat16),
             pltpu.VMEM((nodes, cells), f32),
             pltpu.VMEM((nodes, cells), f32),
             pltpu.VMEM((16, nodes), f32),
+            pltpu.VMEM((32, nodes), jnp.bfloat16),
             pltpu.VMEM((QUAD, 16, cells), f32),
             pltpu.VMEM((ring, 16, cells), f32),
             pltpu.VMEM((16, cells), f32),
@@ -774,7 +841,11 @@
             pltpu.VMEM((ring, 16, cells), f32),
             pltpu.VMEM((QUAD, 16, cells), f32),
             pltpu.VMEM((ring, 16, cells), f32),
-            dma, dma((CHUNKS,)), dma((3,)), dma((3,)), dma((7,)), dma((7,)),
+            pltpu.VMEM((16, cells), f32),
+            pltpu.VMEM((16, cells), f32),
+            pltpu.VMEM((16, cells), f32),
+            pltpu.VMEM((16, cells), f32),
+            dma, dma((CHUNKS,)), dma((3,)), dma((3,)), dma((9,)), dma((9,)),
         ],
         compiler_params=pltpu.CompilerParams(
             collective_id=0, has_side_effects=True, vmem_limit_bytes=16 * 1024 * 1024

time: 32.7 us -> 26.9 us (0.82)
  Pallas kernels: 31.9 us -> 26.2 us
    pallas_call x1, Pallas kernels: 31.1 us -> 25.3 us  [per_device_pair(): pl.pallas_call(functools.partial(step_kernel, nodes * size), out_shape=sh...]
where the time goes in v2:
time: 26.9 us; the launch traced here: 26.8 us
  Pallas kernels  26.2 us (97%)
  between operations  0.64 us (2%)
    pallas_call x1, Pallas kernels, per_device_pair(): pl.pallas_call(functools.partial(step_kernel, nodes * size), out_shape=sh...  25.3 us
    pallas_call x1, Pallas kernels, per_device_pair(): pl.pallas_call(store_kernel, out_shape=shapes, in_specs=[anywhere, anywhe...  0.82 us

profile of v2, /device:TPU:0, one launch (start us, length us, event | category | flops | bytes accessed | tf_op | source)
XLA Modules:
  0.0 26.8 jit_solution(9599492446541584987)
XLA Ops:
  0.6 25.3 %steps.1 = (f32[512,256]{1,0:T(8,128)S(1)}, f32[13,256]{1,0:T(8,128)S(1)}) custom-call(f32[512,256]{1,0:T(8,128)} %f_hbm.1, f32[3,4,256]{2,1,0:T(4,128)} %bitcast.1, s32[4,256]{1,0:T(4,128)} %adj_hbm.1, s32[1,2,256]{2,1,0:T(2,128)} %send_hbm.1), custom_call_target="tpu_custom_call" | custom-call | tf_op jit(solution)/shard_map/steps/pallas_call | solution.py:812
  26.0 0.8 %store.1 = (f32[512,256]{1,0:T(8,128)}, f32[13,256]{1,0:T(8,128)}) custom-call(f32[512,256]{1,0:T(8,128)S(1)} %get-tuple-element.4.state_ref, f32[13,256]{1,0:T(8,128)S(1)} %get-tuple-element.5.fields_ref), custom_call_target="tpu_custom_call" | custom-call | tf_op jit(solution)/shard_map/store/pallas_call | solution.py:856

commit v3 on v2

--- a/solution.py
+++ b/solution.py
@@ -242,9 +242,10 @@
 QUAD = 4
 CHUNKS = 4
 PIECES = 16
-MARKS = (5, 8, 11)
+ISSUE = (1, 4, 1, 0, 0, 1, 1, 1, 1, 1, 1, 16)
+TAKEN = (0, 8, 12, 16)
+PLACES = (2, 2)
 SLABS = 2
-EARLY = 3
 HI = lax.Precision.HIGHEST
 
 
@@ -422,7 +423,7 @@
     f_hbm, n_hbm, adj_hbm, send_hbm,
     out_ref, fields_ref,
     f_ref, n_ref, adj_ref, send_ref, load_s,
-    fx, nx, adjx, sendx, ncat, xn, oh, tr0, wide, fnew, tr1, phi_ref, phi_two,
+    fx, nx, adjx, sendx, ncat, xn, oh, tr0, split, wide, fnew, tr1, phi_ref, phi_parts,
     qb0, zb0, total_mine, total_theirs, qb1, zb1, qb2, zb2, lent0, got0, lent1, got1,
     bulk_s, bulk_r, meta_s, meta_r, stage_s, stage_r,
 ):
@@ -447,6 +448,11 @@
     def z_of(step):
         return lax.rem(me_z + step, ring)
 
+    def lay_rows(ref, moments, extra=None):
+        for r in range(13):
+            row = moments[r] if isinstance(moments, list) else moments[r : r + 1]
+            ref[r] = row if extra is None else row + extra[r]
+
     barrier = pltpu.get_barrier_semaphore()
     for step in range(1, ring):
         pl.semaphore_signal(barrier, inc=1, device_id=at(group, z_of(step), me_q), device_id_type=MESH)
@@ -480,26 +486,56 @@
     for r, row in enumerate(table):
         phi = jnp.where(row_id == r, row, phi)
     phi_ref[...] = phi
-    phi_high = phi.astype(jnp.bfloat16)
-    phi_two[0:16, :] = phi_high
-    phi_two[16:32, :] = (phi - phi_high.astype(jnp.float32)).astype(jnp.bfloat16)
+    rest = phi
+    for i in range(3):
+        leading = rest.astype(jnp.bfloat16)
+        phi_parts[i * 16 : (i + 1) * 16, :] = leading
+        rest = rest - leading.astype(jnp.float32)
+    with jax.named_scope("W_bar"):
+        pl.semaphore_wait(barrier, QUAD + ring - 1)
+
+    def remote(src, dst, s, r, dev):
+        return pltpu.make_async_remote_copy(
+            src_ref=src, dst_ref=dst, send_sem=s, recv_sem=r, device_id=dev, device_id_type=MESH
+        )
+
+    pair = at(other, me_z, me_q)
+
+    piece = nodes // PIECES
+
+    plan, started = iter(ISSUE), []
+
+    def more():
+        first = len(started)
+        last = min(PIECES, first + next(plan))
+        for c in range(first, last):
+            started.append(c)
+            part = pl.ds(c * piece, piece)
+            remote(f_hbm.at[part], fx.at[part], bulk_s, bulk_r.at[sum(c >= t for t in TAKEN) - 1], pair).start()
+
+    metas = [
+        remote(send_hbm, sendx, meta_s.at[0], meta_r.at[0], pair),
+        remote(adj_hbm, adjx, meta_s.at[1], meta_r.at[1], pair),
+        remote(n_hbm, nx, meta_s.at[2], meta_r.at[2], pair),
+    ]
+    for copy in metas:
+        copy.start()
+    more()
+
+    def two_dot(part, state):
+        high = state.astype(jnp.bfloat16)
+        low = (state - high.astype(jnp.float32)).astype(jnp.bfloat16)
+        lead = jnp.dot(phi_parts[:, part], high, preferred_element_type=jnp.float32)
+        tail = jnp.dot(phi_parts[0:32, part], low, preferred_element_type=jnp.float32)
+        return lead[0:16] + (lead[16:32] + tail[0:16]) + (lead[32:48] + tail[16:32])
+
     inv_total = 1.0 / total_vel
     partial = jnp.zeros((16, cells), jnp.float32)
     for c in range(CHUNKS):
         loads[c].wait()
         part = slice(c * rows, (c + 1) * rows)
-        partial = partial + split_dot(phi[:, part], f_ref[part, :])
-    qb0[me_q] = partial * inv_total
-
-    with jax.named_scope("W_bar"):
-        pl.semaphore_wait(barrier, QUAD + ring - 1)
-
-    def remote(src, dst, s, r, dev):
-        return pltpu.make_async_remote_copy(
-            src_ref=src, dst_ref=dst, send_sem=s, recv_sem=r, device_id=dev, device_id_type=MESH
-        )
-
-    pair = at(other, me_z, me_q)
+        partial = partial + two_dot(part, f_ref[part, :])
+    lay_rows(qb0.at[me_q], partial * inv_total)
 
     def in_quad(buffer, i):
         for t in range(1, QUAD):
@@ -523,33 +559,16 @@
     def collect(i, buffer, count):
         with jax.named_scope(f"W_stage{i}"):
             all_of(buffer, stage_r.at[i], count - 1)
-        result = buffer[0]
-        for t in range(1, count):
-            result = result + buffer[t]
-        return result
-
-    piece = nodes // PIECES
-    ratio = PIECES // CHUNKS
-
-    def bulk(first, last):
-        for c in range(first, last):
-            part = pl.ds(c * piece, piece)
-            remote(f_hbm.at[part], fx.at[part], bulk_s, bulk_r.at[c // ratio], pair).start()
-
-    def bulk_wait(c):
-        with jax.named_scope("W_bulk"):
-            part = fx.at[chunk(c)]
-            pltpu.make_async_copy(part, part, bulk_r.at[c]).wait()
-
-    metas = [
-        remote(send_hbm, sendx, meta_s.at[0], meta_r.at[0], pair),
-        remote(adj_hbm, adjx, meta_s.at[1], meta_r.at[1], pair),
-        remote(n_hbm, nx, meta_s.at[2], meta_r.at[2], pair),
-    ]
+        rows13 = []
+        for r in range(13):
+            row = buffer[0, r]
+            for t in range(1, count):
+                row = row + buffer[t, r]
+            rows13.append(row)
+        return rows13
+
     in_quad(qb0, 0)
-    for copy in metas:
-        copy.start()
-    bulk(0, MARKS[0])
+    more()
 
     for copy in small_loads:
         copy.wait()
@@ -582,8 +601,9 @@
     for k in range(faces):
         choose(k, mine, mine, adj_ref[k : k + 1, :])
 
-    zb0[me_z] = collect(0, qb0, QUAD)
+    lay_rows(zb0.at[me_z], collect(0, qb0, QUAD))
     along_z(zb0, 1)
+    more()
 
     with jax.named_scope("W_meta"):
         for copy in metas:
@@ -641,26 +661,26 @@
             parts.append(jnp.exp2(vx_col * (square + slope) + level))
         return jnp.concatenate(parts, axis=0)
 
-    def two_dot(part, state):
-        high = state.astype(jnp.bfloat16)
-        low = (state - high.astype(jnp.float32)).astype(jnp.bfloat16)
-        first = jnp.dot(phi_two[:, part], high, preferred_element_type=jnp.float32)
-        return first[0:16] + first[16:32] + jnp.dot(phi_two[0:16, part], low, preferred_element_type=jnp.float32)
-
     blocks = [(c * (nodes // SLABS), nodes // SLABS) for c in range(SLABS)]
     sent = jnp.zeros((16, cells), jnp.float32)
-    with jax.named_scope("T0p"):
+    with jax.named_scope("T0p_far"):
         for first, count in blocks:
             part = slice(first, first + count)
-            state = f_ref[part, :]
-            lhs = halves(state)
-            tr0[part, mine] = transport(lhs, mine, mine, state, first, count)
-            moved = transport(lhs, mine, far, None, first, count)
+            lhs = halves(f_ref[part, :])
+            split[2 * first : 2 * (first + count), :] = lhs
+            moved = transport(lhs[:count], mine, far, None, first, count)
             tr0[part, far] = moved
             sent = sent + two_dot(part, moved)
-    lent0[...] = sent * (-time_step * inv_total)
+            more()
+    lay_rows(lent0, sent * (-time_step * inv_total))
     across(lent0, got0, 7)
-    bulk(MARKS[0], MARKS[1])
+    more()
+    with jax.named_scope("T0p_mine"):
+        for first, count in blocks:
+            part = slice(first, first + count)
+            lhs = split[2 * first : 2 * (first + count), :]
+            tr0[part, mine] = transport(lhs, mine, mine, f_ref[part, :], first, count)
+            more()
 
     with jax.named_scope("oh2"):
         for k in range(faces):
@@ -668,18 +688,17 @@
             theirs = adjx[k : k + 1, :]
             choose(k, far, far, theirs)
 
-    total_mine[...] = collect(1, zb0, ring)
-    across(total_mine, total_theirs, 2)
-    bulk(MARKS[1], MARKS[2])
-
-    def rows_of(moments):
-        return [moments[r : r + 1] for r in range(13)]
-
-    fields0, own_quad, freq0 = coefficient_rows(rows_of(total_mine[...]))
+    more()
+    fields0, own_quad, freq0 = coefficient_rows(collect(1, zb0, ring))
+    more()
     with jax.named_scope("G_tot0"):
         norm0 = gauss_total(own_quad, cells, z_count) * inv_total
     own_gain = time_step * freq0 * fields0[0] / norm0
     own_keep = 1.0 - time_step * freq0
+    for r, row in enumerate(own_quad + [own_gain, own_keep]):
+        total_mine[r] = row
+    across(total_mine, total_theirs, 2)
+    more()
 
     with jax.named_scope("f1p"):
         for first, count in blocks:
@@ -692,60 +711,56 @@
             away = -time_step * tr0[part, far]
             tr0[part, far] = away
             wide[part, far] = away.astype(jnp.bfloat16)
-        kept = split_dot(phi_ref[...], fnew[...]) * inv_total
+        kept = two_dot(slice(0, nodes), fnew[...]) * inv_total
     arrived(got0, 7)
-    qb1[me_q] = kept + got0[...]
+    lay_rows(qb1.at[me_q], kept, got0)
     in_quad(qb1, 3)
 
     def second_moments(target, leaving):
-        total = jnp.zeros((16, cells), jnp.float32)
-        for first, count in blocks:
-            part = slice(first, first + count)
-            moved = transport(wide[part, :], slice(0, both), target, leaving(part), first, count)
-            total = total + two_dot(part, moved)
-        return total * inv_total
+        part = slice(0, nodes)
+        moved = transport(wide[part, :], slice(0, both), target, leaving(part), 0, nodes)
+        return two_dot(part, moved) * inv_total
 
     with jax.named_scope("T1p_far"):
-        lent1[...] = second_moments(far, lambda part: tr0[part, far])
+        lay_rows(lent1, second_moments(far, lambda part: tr0[part, far]))
     across(lent1, got1, 8)
-    bulk(MARKS[2], PIECES)
+    more()
     with jax.named_scope("T1p_mine"):
         stay = second_moments(mine, lambda part: fnew[part, :])
 
-    zb1[me_z] = collect(3, qb1, QUAD)
-    along_z(zb1, 4)
-
-    arrived(total_theirs, 2)
-    fields_x, their_quad, freq_x = coefficient_rows(rows_of(total_theirs[...]))
-    with jax.named_scope("G_totx"):
-        norm_x = gauss_total(their_quad, cells, z_count) * inv_total
-    their_gain = time_step * freq_x * fields_x[0] / norm_x
-    their_keep = 1.0 - time_step * freq_x
-
-    arrived(got1, 8)
-    qb2[me_q] = stay + got1[...]
-    in_quad(qb2, 5)
-
-    def received(c, carry):
-        bulk_wait(c)
-        part, first = chunk(c), c * rows
+    def received(i):
+        first, last = TAKEN[i] * piece, TAKEN[i + 1] * piece
+        count, part = last - first, slice(first, last)
+        with jax.named_scope("W_bulk"):
+            ref = fx.at[pl.ds(first, count)]
+            pltpu.make_async_copy(ref, ref, bulk_r.at[i]).wait()
+        their_quad = [total_theirs[r] for r in range(10)]
+        their_gain, their_keep = total_theirs[10], total_theirs[11]
         state = fx[part, :]
         lhs = halves(state)
-        here = fnew[part, :] - time_step * transport(lhs, far, mine, None, first, rows)
+        here = fnew[part, :] - time_step * transport(lhs, far, mine, None, first, count)
         there = (
             their_keep * state
-            + (tr0[part, far] - time_step * transport(lhs, far, far, state, first, rows))
-            + their_gain * equilibrium(their_quad, first, rows)
+            + (tr0[part, far] - time_step * transport(lhs[:count], far, far, state, first, count))
+            + their_gain * equilibrium(their_quad, first, count)
         )
         fnew[part, :] = here
         lhs = halves(jnp.concatenate([here, there], axis=1))
-        tr1[part, :] = transport(lhs, slice(0, both), mine, here, first, rows)
-        return carry
-
-    lax.fori_loop(0, EARLY, received, 0)
-    zb2[me_z] = collect(5, qb2, QUAD)
+        tr1[part, :] = transport(lhs, slice(0, both), mine, here, first, count)
+
+    lay_rows(zb1.at[me_z], collect(3, qb1, QUAD))
+    along_z(zb1, 4)
+    arrived(got1, 8)
+    lay_rows(qb2.at[me_q], stay, got1)
+    in_quad(qb2, 5)
+    arrived(total_theirs, 2)
+    for i in range(PLACES[0]):
+        received(i)
+    lay_rows(zb2.at[me_z], collect(5, qb2, QUAD))
     along_z(zb2, 6)
-    mom1 = rows_of(collect(4, zb1, ring))
+    for i in range(PLACES[0], PLACES[1]):
+        received(i)
+    mom1 = collect(4, zb1, ring)
     fields1, quad1, freq1 = coefficient_rows(mom1)
     with jax.named_scope("G_mom1"):
         sums = gauss_moments(quad1, cells, z_count)
@@ -753,7 +768,9 @@
     lift = time_step * freq1 * fields1[0]
     gain1 = lift * inv_sum * float(total_vel)
     keep1 = 1.0 - time_step * freq1
-    lax.fori_loop(EARLY, CHUNKS, received, 0)
+
+    for i in range(PLACES[1], len(TAKEN) - 1):
+        received(i)
 
     def finish(c, carry):
         part = chunk(c)
@@ -767,7 +784,7 @@
     mom_t = collect(6, zb2, ring)
     slope = lift * inv_sum
     last = [
-        keep1 * mom1[r] - time_step * mom_t[r : r + 1] + slope * sums[r] for r in range(13)
+        keep1 * mom1[r] - time_step * mom_t[r] + slope * sums[r] for r in range(13)
     ]
     final = macroscopic_rows(last)
     for r in range(13):
@@ -828,24 +845,25 @@
             pltpu.VMEM((faces + 1, VXY, 2 * cells), f32),
             pltpu.VMEM((faces, 2 * cells, 2 * cells), jnp.bfloat16),
             pltpu.VMEM((nodes, 2 * cells), f32),
+            pltpu.VMEM((2 * nodes, cells), jnp.bfloat16),
             pltpu.VMEM((nodes, 2 * cells), jnp.bfloat16),
             pltpu.VMEM((nodes, cells), f32),
             pltpu.VMEM((nodes, cells), f32),
             pltpu.VMEM((16, nodes), f32),
-            pltpu.VMEM((32, nodes), jnp.bfloat16),
-            pltpu.VMEM((QUAD, 16, cells), f32),
-            pltpu.VMEM((ring, 16, cells), f32),
-            pltpu.VMEM((16, cells), f32),
-            pltpu.VMEM((16, cells), f32),
-            pltpu.VMEM((QUAD, 16, cells), f32),
-            pltpu.VMEM((ring, 16, cells), f32),
-            pltpu.VMEM((QUAD, 16, cells), f32),
-            pltpu.VMEM((ring, 16, cells), f32),
-            pltpu.VMEM((16, cells), f32),
-            pltpu.VMEM((16, cells), f32),
-            pltpu.VMEM((16, cells), f32),
-            pltpu.VMEM((16, cells), f32),
-            dma, dma((CHUNKS,)), dma((3,)), dma((3,)), dma((9,)), dma((9,)),
+            pltpu.VMEM((48, nodes), jnp.bfloat16),
+            pltpu.VMEM((QUAD, 13, 1, cells), f32),
+            pltpu.VMEM((ring, 13, 1, cells), f32),
+            pltpu.VMEM((12, 1, cells), f32),
+            pltpu.VMEM((12, 1, cells), f32),
+            pltpu.VMEM((QUAD, 13, 1, cells), f32),
+            pltpu.VMEM((ring, 13, 1, cells), f32),
+            pltpu.VMEM((QUAD, 13, 1, cells), f32),
+            pltpu.VMEM((ring, 13, 1, cells), f32),
+            pltpu.VMEM((13, 1, cells), f32),
+            pltpu.VMEM((13, 1, cells), f32),
+            pltpu.VMEM((13, 1, cells), f32),
+            pltpu.VMEM((13, 1, cells), f32),
+            dma, dma((len(TAKEN) - 1,)), dma((3,)), dma((3,)), dma((9,)), dma((9,)),
         ],
         compiler_params=pltpu.CompilerParams(
             collective_id=0, has_side_effects=True, vmem_limit_bytes=16 * 1024 * 1024

time: 26.9 us -> 26 us (0.967)
  Pallas kernels: 26.2 us -> 25.2 us
    pallas_call x1, Pallas kernels: 25.3 us -> 24.4 us  [per_device_pair(): pl.pallas_call(functools.partial(step_kernel, nodes * size), out_shape=sh...]
where the time goes in v3:
time: 26 us; the launch traced here: 25.8 us
  Pallas kernels  25.2 us (97%)
  between operations  0.64 us (2%)
    pallas_call x1, Pallas kernels, per_device_pair(): pl.pallas_call(functools.partial(step_kernel, nodes * size), out_shape=sh...  24.4 us
    pallas_call x1, Pallas kernels, per_device_pair(): pl.pallas_call(store_kernel, out_shape=shapes, in_specs=[anywhere, anywhe...  0.82 us

profile of v3, /device:TPU:0, one launch (start us, length us, event | category | flops | bytes accessed | tf_op | source)
XLA Modules:
  0.0 25.8 jit_solution(6331820221541204622)
XLA Ops:
  0.6 24.4 %steps.1 = (f32[512,256]{1,0:T(8,128)S(1)}, f32[13,256]{1,0:T(8,128)S(1)}) custom-call(f32[512,256]{1,0:T(8,128)} %f_hbm.1, f32[3,4,256]{2,1,0:T(4,128)} %bitcast.1, s32[4,256]{1,0:T(4,128)} %adj_hbm.1, s32[1,2,256]{2,1,0:T(2,128)} %send_hbm.1), custom_call_target="tpu_custom_call" | custom-call | tf_op jit(solution)/shard_map/steps/pallas_call | solution.py:829
  25.0 0.8 %store.1 = (f32[512,256]{1,0:T(8,128)}, f32[13,256]{1,0:T(8,128)}) custom-call(f32[512,256]{1,0:T(8,128)S(1)} %get-tuple-element.4.state_ref, f32[13,256]{1,0:T(8,128)S(1)} %get-tuple-element.5.fields_ref), custom_call_target="tpu_custom_call" | custom-call | tf_op jit(solution)/shard_map/store/pallas_call | solution.py:874

commit v4 on v3

--- a/solution.py
+++ b/solution.py
@@ -379,43 +379,69 @@
                 acc = acc + plus * horner(even, delta)
         return acc
 
-    acc = lax.fori_loop(0, VXY // 8, block, jnp.zeros((8, width), jnp.float32))
+    acc = jnp.zeros((8, width), jnp.float32)
+    for b in range(VXY // 8):
+        acc = block(b, acc)
     return jnp.sum(acc, axis=0, keepdims=True)
 
 
-def gauss_moments(q, width, z_count):
+def column_weights(block):
+    k = lax.broadcasted_iota(jnp.int32, (1, 8 * VXY), 1)
+    x = ((k & 7) + block * 8).astype(jnp.float32) - (VXY - 1) / 2.0
+    y = (k >> 4).astype(jnp.float32) + 0.5
+    y = jnp.where((k & 8) == 0, y, -y)
+    square = x * x + y * y
+    rows = [jnp.ones_like(x), x, y, x * x, y * y, x * y, x * square, y * square]
+    row_id = lax.broadcasted_iota(jnp.int32, (8, 8 * VXY), 0)
+    table = jnp.zeros((8, 8 * VXY), jnp.float32)
+    for r, row in enumerate(rows):
+        table = jnp.where(row_id == r, row, table)
+    high = table.astype(jnp.bfloat16).astype(jnp.float32)
+    return jnp.concatenate([high, table - high], axis=0).astype(jnp.bfloat16)
+
+
+def gauss_moments(q, width, z_count, weights_ref):
     levels = level_coefficients(q, z_count, 4)
-    zero = jnp.zeros((8, width), jnp.float32)
+    half = z_count // 2
+    zero = jnp.zeros((16, width), jnp.float32)
 
     def block(b, carry):
-        sums = [[zero] * n for n in (4, 3, 2, 1)]
-        for vx, vy, ((p_up, d_up, x_up), (p_down, d_down, x_down)) in gauss_columns(q, width, b):
-            for c in range(4):
-                above = (d_up if c % 2 else p_up) * horner(levels[c], x_up)
-                below = (d_down if c % 2 else p_down) * horner(levels[c], x_down)
-                both = above + below
-                sums[c][0] = sums[c][0] + both
-                if c < 3:
-                    diff = (above - below) * vy
-                    sums[c][1] = sums[c][1] + diff
-                if c < 2:
-                    sums[c][2] = sums[c][2] + both * (vy * vy)
-                if c < 1:
-                    sums[c][3] = sums[c][3] + diff * (vy * vy)
-        (s0, s1, s2, s3), (z0, z1, z2), (zz0, zz1), (zc,) = sums
-        vxx = vx * vx
-        new = (
-            s0, vx * s0, s1, z0, vxx * s0, s2, zz0, vx * s1, vx * z0, z1,
-            vx * (vxx * s0 + s2 + zz0), vxx * s1 + s3 + zz1, vxx * z0 + z2 + zc,
-        )
-        return tuple(x + y for x, y in zip(carry, new))
-
-    terms = lax.fori_loop(0, VXY // 8, block, (zero,) * 13)
-    return [jnp.sum(t, axis=0, keepdims=True) for t in terms]
-
-
-def split_dot(lhs, rhs):
-    return jnp.dot(lhs, rhs, precision=HI, preferred_element_type=jnp.float32)
+        tiles = [[] for _ in range(2 * half + 1)]
+        for _, _, ((p_up, d_up, x_up), (p_down, d_down, x_down)) in gauss_columns(q, width, b):
+            plus = jnp.concatenate([p_up, p_down], axis=0)
+            diff = jnp.concatenate([d_up, d_down], axis=0)
+            delta = jnp.concatenate([x_up, x_down], axis=0)
+            for j in range(half):
+                lead = plus.astype(jnp.bfloat16)
+                tiles[j].append(lead)
+                tiles[half + j].append(diff.astype(jnp.bfloat16))
+                if j == 0:
+                    tiles[2 * half].append((plus - lead.astype(jnp.float32)).astype(jnp.bfloat16))
+                if j < half - 1:
+                    plus, diff = plus * delta, diff * delta
+        weights = weights_ref[b]
+        sums = [
+            jnp.dot(weights, jnp.concatenate(t, axis=0), preferred_element_type=jnp.float32) for t in tiles
+        ]
+        sums[0] = sums[0] + sums.pop()
+        return tuple(x + y for x, y in zip(carry, sums))
+
+    sums = (zero,) * (2 * half)
+    for b in range(VXY // 8):
+        sums = block(b, sums)
+    sums = [t[:8] + t[8:] for t in sums]
+    m0, m1, m2, m3 = [
+        sum(levels[c][j] * sums[(c % 2) * half + j] for j in range(half)) for c in range(4)
+    ]
+    h = spacing
+    row = lambda m, r: m[r : r + 1]
+    return [
+        row(m0, 0), h * row(m0, 1), h * row(m0, 2), row(m1, 0),
+        h * h * row(m0, 3), h * h * row(m0, 4), row(m2, 0),
+        h * h * row(m0, 5), h * row(m1, 1), h * row(m1, 2),
+        h * (h * h * row(m0, 6) + row(m2, 1)), h * (h * h * row(m0, 7) + row(m2, 2)),
+        h * h * (row(m1, 3) + row(m1, 4)) + row(m3, 0),
+    ]
 
 
 def step_kernel(
@@ -423,7 +449,7 @@
     f_hbm, n_hbm, adj_hbm, send_hbm,
     out_ref, fields_ref,
     f_ref, n_ref, adj_ref, send_ref, load_s,
-    fx, nx, adjx, sendx, ncat, xn, oh, tr0, split, wide, fnew, tr1, phi_ref, phi_parts,
+    fx, nx, adjx, sendx, ncat, xn, oh, tr0, split, wide, fnew, tr1, phi_parts, weights,
     qb0, zb0, total_mine, total_theirs, qb1, zb1, qb2, zb2, lent0, got0, lent1, got1,
     bulk_s, bulk_r, meta_s, meta_r, stage_s, stage_r,
 ):
@@ -458,7 +484,8 @@
         pl.semaphore_signal(barrier, inc=1, device_id=at(group, z_of(step), me_q), device_id_type=MESH)
     for step in range(1, QUAD):
         pl.semaphore_signal(barrier, inc=1, device_id=at(group, me_z, q_of(step)), device_id_type=MESH)
-    pl.semaphore_signal(barrier, inc=1, device_id=at(other, me_z, me_q), device_id_type=MESH)
+    for step in range(QUAD):
+        pl.semaphore_signal(barrier, inc=1, device_id=at(other, me_z, q_of(step)), device_id_type=MESH)
 
     def chunk(c):
         return pl.ds(pl.multiple_of(c * rows, rows), rows)
@@ -485,14 +512,13 @@
     phi = jnp.zeros((16, nodes), jnp.float32)
     for r, row in enumerate(table):
         phi = jnp.where(row_id == r, row, phi)
-    phi_ref[...] = phi
     rest = phi
     for i in range(3):
         leading = rest.astype(jnp.bfloat16)
         phi_parts[i * 16 : (i + 1) * 16, :] = leading
         rest = rest - leading.astype(jnp.float32)
     with jax.named_scope("W_bar"):
-        pl.semaphore_wait(barrier, QUAD + ring - 1)
+        pl.semaphore_wait(barrier, 2 * QUAD + ring - 2)
 
     def remote(src, dst, s, r, dev):
         return pltpu.make_async_remote_copy(
@@ -601,6 +627,8 @@
     for k in range(faces):
         choose(k, mine, mine, adj_ref[k : k + 1, :])
 
+    for b in range(VXY // 8):
+        weights[b] = column_weights(b)
     lay_rows(zb0.at[me_z], collect(0, qb0, QUAD))
     along_z(zb0, 1)
     more()
@@ -723,7 +751,8 @@
 
     with jax.named_scope("T1p_far"):
         lay_rows(lent1, second_moments(far, lambda part: tr0[part, far]))
-    across(lent1, got1, 8)
+    for t in range(QUAD):
+        remote(lent1, got1.at[me_q], stage_s.at[8], stage_r.at[8], at(other, me_z, q_of(t))).start()
     more()
     with jax.named_scope("T1p_mine"):
         stay = second_moments(mine, lambda part: fnew[part, :])
@@ -748,22 +777,23 @@
         lhs = halves(jnp.concatenate([here, there], axis=1))
         tr1[part, :] = transport(lhs, slice(0, both), mine, here, first, count)
 
+    lay_rows(qb2.at[me_q], stay)
+    in_quad(qb2, 5)
     lay_rows(zb1.at[me_z], collect(3, qb1, QUAD))
     along_z(zb1, 4)
-    arrived(got1, 8)
-    lay_rows(qb2.at[me_q], stay, got1)
-    in_quad(qb2, 5)
     arrived(total_theirs, 2)
     for i in range(PLACES[0]):
         received(i)
-    lay_rows(zb2.at[me_z], collect(5, qb2, QUAD))
+    arrived(got1, 8)
+    from_far = [got1[0, r] + got1[1, r] + (got1[2, r] + got1[3, r]) for r in range(13)]
+    lay_rows(zb2.at[me_z], collect(5, qb2, QUAD), from_far)
     along_z(zb2, 6)
     for i in range(PLACES[0], PLACES[1]):
         received(i)
     mom1 = collect(4, zb1, ring)
     fields1, quad1, freq1 = coefficient_rows(mom1)
     with jax.named_scope("G_mom1"):
-        sums = gauss_moments(quad1, cells, z_count)
+        sums = gauss_moments(quad1, cells, z_count, weights)
     inv_sum = 1.0 / sums[0]
     lift = time_step * freq1 * fields1[0]
     gain1 = lift * inv_sum * float(total_vel)
@@ -793,7 +823,7 @@
         pltpu.make_async_copy(fx, fx, bulk_s).wait()
         for copy in metas:
             copy.wait_send()
-        for i, buffer in ((2, total_mine), (7, lent0), (8, lent1)):
+        for i, buffer in ((2, total_mine), (7, lent0), (8, got1)):
             pltpu.make_async_copy(buffer, buffer, stage_s.at[i]).wait()
         for i, buffer, count in (
             (0, qb0, QUAD), (1, zb0, ring), (3, qb1, QUAD), (4, zb1, ring), (5, qb2, QUAD), (6, zb2, ring),
@@ -849,8 +879,8 @@
             pltpu.VMEM((nodes, 2 * cells), jnp.bfloat16),
             pltpu.VMEM((nodes, cells), f32),
             pltpu.VMEM((nodes, cells), f32),
-            pltpu.VMEM((16, nodes), f32),
             pltpu.VMEM((48, nodes), jnp.bfloat16),
+            pltpu.VMEM((VXY // 8, 16, 8 * VXY), jnp.bfloat16),
             pltpu.VMEM((QUAD, 13, 1, cells), f32),
             pltpu.VMEM((ring, 13, 1, cells), f32),
             pltpu.VMEM((12, 1, cells), f32),
@@ -862,7 +892,7 @@
             pltpu.VMEM((13, 1, cells), f32),
             pltpu.VMEM((13, 1, cells), f32),
             pltpu.VMEM((13, 1, cells), f32),
-            pltpu.VMEM((13, 1, cells), f32),
+            pltpu.VMEM((QUAD, 13, 1, cells), f32),
             dma, dma((len(TAKEN) - 1,)), dma((3,)), dma((3,)), dma((9,)), dma((9,)),
         ],
         compiler_params=pltpu.CompilerParams(

time: 26 us -> 24.3 us (0.935)
  Pallas kernels: 25.2 us -> 23.5 us
    pallas_call x1, Pallas kernels: 24.4 us -> 22.7 us  [per_device_pair(): pl.pallas_call(functools.partial(step_kernel, nodes * size), out_shape=sh...]
where the time goes in v4:
time: 24.3 us; the launch traced here: 24.2 us
  Pallas kernels  23.5 us (97%)
  between operations  0.64 us (3%)
    pallas_call x1, Pallas kernels, per_device_pair(): pl.pallas_call(functools.partial(step_kernel, nodes * size), out_shape=sh...  22.7 us
    pallas_call x1, Pallas kernels, per_device_pair(): pl.pallas_call(store_kernel, out_shape=shapes, in_specs=[anywhere, anywhe...  0.82 us

profile of v4, /device:TPU:0, one launch (start us, length us, event | category | flops | bytes accessed | tf_op | source)
XLA Modules:
  0.0 24.2 jit_solution(10130955183130004688)
XLA Ops:
  0.6 22.7 %steps.1 = (f32[512,256]{1,0:T(8,128)S(1)}, f32[13,256]{1,0:T(8,128)S(1)}) custom-call(f32[512,256]{1,0:T(8,128)} %f_hbm.1, f32[3,4,256]{2,1,0:T(4,128)} %bitcast.1, s32[4,256]{1,0:T(4,128)} %adj_hbm.1, s32[1,2,256]{2,1,0:T(2,128)} %send_hbm.1), custom_call_target="tpu_custom_call" | custom-call | tf_op jit(solution)/shard_map/steps/pallas_call | solution.py:859
  23.4 0.8 %store.1 = (f32[512,256]{1,0:T(8,128)}, f32[13,256]{1,0:T(8,128)}) custom-call(f32[512,256]{1,0:T(8,128)S(1)} %get-tuple-element.4.state_ref, f32[13,256]{1,0:T(8,128)S(1)} %get-tuple-element.5.fields_ref), custom_call_target="tpu_custom_call" | custom-call | tf_op jit(solution)/shard_map/store/pallas_call | solution.py:904

commit v5 on v4

--- a/solution.py
+++ b/solution.py
@@ -799,18 +799,20 @@
     gain1 = lift * inv_sum * float(total_vel)
     keep1 = 1.0 - time_step * freq1
 
+
+    def finish(i):
+        first, last = TAKEN[i] * piece, TAKEN[i + 1] * piece
+        part = slice(first, last)
+        out_ref[part, :] = (
+            keep1 * fnew[part, :] - time_step * tr1[part, :] + gain1 * equilibrium(quad1, first, last - first)
+        )
+
+    with jax.named_scope("fin"):
+        for i in range(PLACES[1]):
+            finish(i)
     for i in range(PLACES[1], len(TAKEN) - 1):
         received(i)
-
-    def finish(c, carry):
-        part = chunk(c)
-        out_ref[part, :] = (
-            keep1 * fnew[part, :] - time_step * tr1[part, :] + gain1 * equilibrium(quad1, c * rows, rows)
-        )
-        return carry
-
-    with jax.named_scope("fin"):
-        lax.fori_loop(0, CHUNKS, finish, 0)
+        finish(i)
     mom_t = collect(6, zb2, ring)
     slope = lift * inv_sum
     last = [

time: 24.3 us -> 24.2 us (level)
  no operation moved by 1% of the time
where the time goes in v5:
time: 24.2 us; the launch traced here: 24 us
  Pallas kernels  23.4 us (97%)
  between operations  0.64 us (3%)
    pallas_call x1, Pallas kernels, per_device_pair(): pl.pallas_call(functools.partial(step_kernel, nodes * size), out_shape=sh...  22.6 us
    pallas_call x1, Pallas kernels, per_device_pair(): pl.pallas_call(store_kernel, out_shape=shapes, in_specs=[anywhere, anywhe...  0.82 us

profile of v5, /device:TPU:0, one launch (start us, length us, event | category | flops | bytes accessed | tf_op | source)
XLA Modules:
  0.0 24.0 jit_solution(7608801153750460677)
XLA Ops:
  0.6 22.6 %steps.1 = (f32[512,256]{1,0:T(8,128)S(1)}, f32[13,256]{1,0:T(8,128)S(1)}) custom-call(f32[512,256]{1,0:T(8,128)} %f_hbm.1, f32[3,4,256]{2,1,0:T(4,128)} %bitcast.1, s32[4,256]{1,0:T(4,128)} %adj_hbm.1, s32[1,2,256]{2,1,0:T(2,128)} %send_hbm.1), custom_call_target="tpu_custom_call" | custom-call | tf_op jit(solution)/shard_map/steps/pallas_call | solution.py:861
  23.2 0.8 %store.1 = (f32[512,256]{1,0:T(8,128)}, f32[13,256]{1,0:T(8,128)}) custom-call(f32[512,256]{1,0:T(8,128)S(1)} %get-tuple-element.4.state_ref, f32[13,256]{1,0:T(8,128)S(1)} %get-tuple-element.5.fields_ref), custom_call_target="tpu_custom_call" | custom-call | tf_op jit(solution)/shard_map/store/pallas_call | solution.py:906

commit v6 on v5

--- a/solution.py
+++ b/solution.py
@@ -767,15 +767,29 @@
         their_gain, their_keep = total_theirs[10], total_theirs[11]
         state = fx[part, :]
         lhs = halves(state)
-        here = fnew[part, :] - time_step * transport(lhs, far, mine, None, first, count)
         there = (
             their_keep * state
             + (tr0[part, far] - time_step * transport(lhs[:count], far, far, state, first, count))
             + their_gain * equilibrium(their_quad, first, count)
         )
+        stacked = jnp.concatenate([lhs, halves(there)], axis=0)
+        subs = range(count // VXY)
+        speeds = [line_velocity(first + sub * VXY) for sub in subs]
+        once, twice = [None] * len(subs), [None] * len(subs)
+        for k in range(faces):
+            got = jnp.dot(stacked, oh[k, far, mine], preferred_element_type=jnp.float32)
+            for sub in subs:
+                vy, vz = speeds[sub]
+                speed = xn[k, :, mine] + (vy * ncat[1, k : k + 1, mine] + vz * ncat[2, k : k + 1, mine])
+                inward = jnp.minimum(speed, 0.0)
+                low, high = sub * VXY, (sub + 1) * VXY
+                before = inward * (got[low:high] + got[count + low : count + high])
+                after = inward * (got[2 * count + low : 2 * count + high] + got[3 * count + low : 3 * count + high])
+                once[sub] = before if once[sub] is None else once[sub] + before
+                twice[sub] = after if twice[sub] is None else twice[sub] + after
+        here = fnew[part, :] - time_step * jnp.concatenate(once, axis=0)
         fnew[part, :] = here
-        lhs = halves(jnp.concatenate([here, there], axis=1))
-        tr1[part, :] = transport(lhs, slice(0, both), mine, here, first, count)
+        tr1[part, :] = jnp.concatenate(twice, axis=0) + transport(halves(here), mine, mine, here, first, count)
 
     lay_rows(qb2.at[me_q], stay)
     in_quad(qb2, 5)

time: 24.2 us -> 24.2 us (level)
  no operation moved by 1% of the time
where the time goes in v6:
time: 24.2 us; the launch traced here: 24.1 us
  Pallas kernels  23.4 us (97%)
  between operations  0.64 us (3%)
    pallas_call x1, Pallas kernels, per_device_pair(): pl.pallas_call(functools.partial(step_kernel, nodes * size), out_shape=sh...  22.6 us
    pallas_call x1, Pallas kernels, per_device_pair(): pl.pallas_call(store_kernel, out_shape=shapes, in_specs=[anywhere, anywhe...  0.82 us

profile of v6, /device:TPU:0, one launch (start us, length us, event | category | flops | bytes accessed | tf_op | source)
XLA Modules:
  0.0 24.1 jit_solution(5229999585734827708)
XLA Ops:
  0.6 22.6 %steps.1 = (f32[512,256]{1,0:T(8,128)S(1)}, f32[13,256]{1,0:T(8,128)S(1)}) custom-call(f32[512,256]{1,0:T(8,128)} %f_hbm.1, f32[3,4,256]{2,1,0:T(4,128)} %bitcast.1, s32[4,256]{1,0:T(4,128)} %adj_hbm.1, s32[1,2,256]{2,1,0:T(2,128)} %send_hbm.1), custom_call_target="tpu_custom_call" | custom-call | tf_op jit(solution)/shard_map/steps/pallas_call | solution.py:875
  23.2 0.8 %store.1 = (f32[512,256]{1,0:T(8,128)}, f32[13,256]{1,0:T(8,128)}) custom-call(f32[512,256]{1,0:T(8,128)S(1)} %get-tuple-element.4.state_ref, f32[13,256]{1,0:T(8,128)S(1)} %get-tuple-element.5.fields_ref), custom_call_target="tpu_custom_call" | custom-call | tf_op jit(solution)/shard_map/store/pallas_call | solution.py:920
